TPU v7x, 512 devices: a whole 4x4x16 slice. The times are simulated.
512 devices in a mesh: tm: 64 (over x, z), tile: 8 (over y, core).
Axes of the slice: x: 4, y: 4, z: 16, core: 2. Of those that a mesh axis runs over, the one named last changes fastest.
Arguments:
- movie_frames: bfloat16 [64, 1024, 1024], P('tm', None, 'tile'), may hold values from -6 to 6
- patch_weight: bfloat16 [64, 128], replicated, may hold values from -0.75 to 0.75
- depth_weight: bfloat16 [3, 3, 3, 128], replicated, may hold values from -4 to 4
- point_weight: bfloat16 [3, 128, 128], replicated, may hold values from -0.5 to 0.5
- observe_weight: bfloat16 [16, 16, 128, 256], P('tile'), may hold values from -0.03125 to 0.03125
- input_map: float32 [256, 256], replicated, may hold values from -0.375 to 0.375
- mode_decay: float32 [128], replicated, may hold values from 0.86 to 1, as said below
- mode_angle: float32 [128], replicated, may hold values from -0.1 to 0.1
- smooth_decay: float32 [128], replicated, may hold values from 0.86 to 1, as said below
- smooth_angle: float32 [128], replicated, may hold values from -0.1 to 0.1
- readout: float32 [256, 256], replicated, may hold values from -0.375 to 0.375
Outputs:
- latent: float32 [64, 256], P('tm', 'tile')
Inputs may be any that keep to these rules, and one draw needn't show every extreme that they name: `mode_decay`: every mode's magnitude per frame lies strictly below one. `smooth_decay`: every mode's gain magnitude per frame lies strictly below one.
All inputs are finite; a program needn't handle non-finite values.
Results may differ from a plain program's by a relative error of at most 0.00075.
Values may be sent and summed in bfloat16 or wider, within the bound.
No kernel may reach another device: no remote copies, remote signals or barrier semaphores. Data moves between devices by JAX's collectives and lax.ppermute only.
A program may use at most 64 MiB of HBM per device.

v0:
```python
import jax
import jax.numpy as jnp
from jax import lax
from jax.sharding import PartitionSpec as P

PATCH = 8
POOL = 8
LAYERS = 3


def entering(x, axis, combine, identity, reverse):
    length, position = (lax.axis_size(axis), lax.axis_index(axis))
    everything = jax.tree.map(lambda part: lax.all_gather(part, axis), x)
    start = jax.tree.map(
        lambda part, zero: jnp.broadcast_to(jnp.asarray(zero, part.dtype), part.shape), x, identity
    )

    def turn(k, before):
        at = length - 1 - k if reverse else k
        reached = at > position if reverse else at < position
        new = combine(before, jax.tree.map(lambda part: part[at], everything))
        return jax.tree.map(lambda a, b: jnp.where(reached, a, b), new, before)

    return lax.fori_loop(0, length, turn, start)


def with_halo(x, sides, width):
    for axis, dim in sides:
        size, length = (lax.axis_size(axis), x.shape[dim])
        up = [(i, (i + 1) % size) for i in range(size - 1)]
        down = [(j, i) for i, j in up]
        last = lax.slice_in_dim(x, length - width, length, axis=dim)
        initial = lax.slice_in_dim(x, 0, width, axis=dim)
        before = lax.ppermute(last, axis, up)
        after = lax.ppermute(initial, axis, down)
        x = jnp.concatenate([before, x, after], axis=dim)
    return x


def rotate(state, magnitude, cosine, sine):
    real_part = state[..., 0]
    imag_part = state[..., 1]
    return jnp.stack(
        [
            magnitude * (cosine * real_part - sine * imag_part),
            magnitude * (sine * real_part + cosine * imag_part),
        ],
        axis=-1,
    )


def run_chain(inputs, magnitude, cosine, sine, initial, backward):

    def advance(state, element):
        updated = rotate(state, magnitude, cosine, sine) + element
        return (updated, updated)

    final_state, states = lax.scan(advance, initial, inputs, reverse=backward)
    return states


def make_compose(magnitude, angles, frame_count):

    def compose(earlier, latter):
        earlier_count, earlier_state = earlier
        latter_count, latter_state = latter
        steps = latter_count[0] * frame_count
        factor = magnitude**steps
        moved = rotate(earlier_state, factor, jnp.cos(steps * angles), jnp.sin(steps * angles))
        return (earlier_count + latter_count, moved + latter_state)

    return compose


def forward_entry(summary, magnitude, angles, frame_count):
    compose = make_compose(magnitude, angles, frame_count)
    identity = (jnp.zeros((1,), jnp.float32), jnp.zeros_like(summary))
    prefix = entering((jnp.ones((1,), jnp.float32), summary), "tm", compose, identity, False)
    return prefix[1]


def backward_entry(summary, magnitude, angles, frame_count):
    compose = make_compose(magnitude, angles, frame_count)
    identity = (jnp.zeros((1,), jnp.float32), jnp.zeros_like(summary))
    prefix = entering((jnp.ones((1,), jnp.float32), summary), "tm", compose, identity, True)
    return prefix[1]


def block_chain(inputs, magnitude, angles, backward, direction):
    frame_count = inputs.shape[0]
    cosine = jnp.cos(angles)
    sine = jnp.sin(angles)
    zero_state = jnp.zeros(inputs.shape[1:], jnp.float32)
    local_states = run_chain(inputs, magnitude, cosine, sine, zero_state, backward)
    if direction == "forward":
        incoming = forward_entry(local_states[-1], magnitude, angles, frame_count)
    else:
        incoming = backward_entry(local_states[0], magnitude, angles, frame_count)
    return run_chain(inputs, magnitude, cosine, sine, incoming, backward)


def embed(frames, patch_weight):
    frame_count, height, width = frames.shape
    grid_rows = height // PATCH
    grid_cols = width // PATCH
    patches = (
        frames.reshape(frame_count, grid_rows, PATCH, grid_cols, PATCH)
        .transpose(0, 1, 3, 2, 4)
        .reshape(frame_count, grid_rows, grid_cols, PATCH * PATCH)
    )
    return jax.nn.gelu(jnp.dot(patches, patch_weight, preferred_element_type=jnp.float32)).astype(
        jnp.bfloat16
    )


def conv_layer(hidden, padded, depth_weight, point_weight, layer_index):
    grid_rows = hidden.shape[1]
    grid_cols = hidden.shape[2]
    summed = jnp.zeros(hidden.shape, jnp.float32)
    for row_shift in range(3):
        for col_shift in range(3):
            kernel = depth_weight[layer_index, row_shift, col_shift].astype(jnp.float32)
            summed = (
                summed
                + padded[
                    :, row_shift : row_shift + grid_rows, col_shift : col_shift + grid_cols
                ].astype(jnp.float32)
                * kernel
            )
    depthwise = summed.astype(jnp.bfloat16)
    branch = jax.nn.gelu(
        jnp.dot(depthwise, point_weight[layer_index], preferred_element_type=jnp.float32)
    )
    return (hidden.astype(jnp.float32) + branch).astype(jnp.bfloat16)


def shards(
    movie_frames,
    patch_weight,
    depth_weight,
    point_weight,
    observe_weight,
    input_map,
    mode_decay,
    mode_angle,
    smooth_decay,
    smooth_angle,
    readout,
):
    frame_count, height, width = movie_frames.shape
    grid_rows = height // PATCH
    grid_cols = width // PATCH
    channels = patch_weight.shape[1]
    tile_count = lax.axis_size("tile")
    tile_index = lax.axis_index("tile")
    hidden = embed(movie_frames, patch_weight)
    for layer_index in range(LAYERS):
        widened = with_halo(hidden, (("tile", 2),), 1)
        padded = jnp.pad(widened, ((0, 0), (1, 1), (0, 0), (0, 0)))
        hidden = conv_layer(hidden, padded, depth_weight, point_weight, layer_index)
    pooled = jnp.mean(
        hidden.astype(jnp.float32).reshape(
            frame_count, grid_rows // POOL, POOL, grid_cols // POOL, POOL, channels
        ),
        axis=(2, 4),
    ).astype(jnp.bfloat16)
    features = pooled.transpose(0, 2, 1, 3).reshape(frame_count, -1)
    partial_value = jnp.dot(
        features,
        observe_weight.reshape(-1, observe_weight.shape[-1]),
        preferred_element_type=jnp.float32,
    )
    latent_share = readout.shape[0] // tile_count
    observed = lax.psum(partial_value, "tile")
    drive = jnp.dot(observed, input_map.T, precision=lax.Precision.HIGHEST)
    magnitude, angles = (mode_decay, mode_angle)
    back_magnitude, back_angles = (smooth_decay, smooth_angle)
    mode_count = magnitude.shape[0]
    drive = (
        drive.reshape(frame_count, mode_count, 2) * jnp.sqrt(1.0 - magnitude * magnitude)[:, None]
    )
    filtered = block_chain(drive, magnitude, angles, False, "forward")
    weighted = filtered * jnp.sqrt(1.0 - back_magnitude * back_magnitude)[:, None]
    smoothed = block_chain(weighted, back_magnitude, back_angles, True, "backward")
    smoothed_flat = smoothed.reshape(frame_count, 2 * mode_count)
    latent_rows = lax.dynamic_slice_in_dim(readout, tile_index * latent_share, latent_share, 0)
    return jnp.dot(smoothed_flat, latent_rows.T, precision=lax.Precision.HIGHEST)


def solution(mesh):
    placed = (
        P("tm", None, "tile"),
        P(),
        P(),
        P(),
        P("tile", None, None, None),
        P(),
        P(),
        P(),
        P(),
        P(),
        P(),
    )
    return jax.shard_map(
        shards, mesh=mesh, in_specs=placed, out_specs=P("tm", "tile"), check_vma=False
    )
```

profile of v0, /device:TPU:4, one launch (start us, length us, event | category | flops | bytes accessed | tf_op | source)
XLA Modules:
  0.0 549.2 jit_solution(16845307529792666886)
XLA Ops:
  0.0 7.0 %reshape.321 = bf16[1,128,8,16,8]{4,3,2,1,0:T(8,128)(2,1)} reshape(bf16[1,1024,128]{2,1,0:T(8,128)(2,1)} %param.15) | data formatting | bytes 524288 | tf_op jit(solution)/shard_map/reshape | solution.py:107
  7.0 5.4 copy.18
  13.0 1.9 collective-permute-start
  14.8 1.3 collective-permute-start.1
  16.3 3.1 collective-permute-done.1
  19.5 1.4 fusion.18
  21.0 4.5 collective-permute-start.2
  25.5 1.3 collective-permute-start.3
  26.9 1.7 collective-permute-done.3
  28.8 1.4 fusion.26
  30.3 4.1 collective-permute-start.4
  34.4 1.3 collective-permute-start.5
  35.9 1.3 dynamic-slice
  37.3 0.8 dynamic-update-slice
  38.1 128.0 %all-reduce.3 = f32[64]{0:T(128)S(1)} all-reduce(f32[64]{0:T(128)S(1)} %dynamic-update-slice), channel_id=1, replica_groups=mesh['tm'=64,'tile'=8] {'tm'}, use_global_device_ids=true, to_apply=%add.3 | all-reduce | flops 64 | bytes 512
  166.3 1.5 fusion.34
  168.3 12.8 %psum.7 = f32[256]{0:T(256)S(1)} all-reduce(f32[256]{0:T(256)S(1)} %bitcast.333), channel_id=1, replica_groups=mesh['tm'=64,'tile'=8] {'tile'}, use_global_device_ids=true, to_apply=%region_1.2 | all-reduce | flops 256 | bytes 2048 | tf_op jit(solution)/shard_map/psum | solution.py:174
  181.4 98.4 %all-gather = f32[8192,2]{0,1:T(2,128)S(1)} all-gather(f32[128,2]{0,1:T(2,128)S(1)} %maximum_add_fusion.3), channel_id=2, replica_groups=mesh['tm'=64,'tile'=8] {'tm'}, dimensions={0}, use_global_device_ids=true | all-gather | bytes 66560 | tf_op jit(solution)/shard_map/all_gather | solution.py:13
  279.8 93.2 %while.20 = (s32[]{:T(128)}, f32[128,2]{0,1:T(2,128)S(1)}, s32[]{:T(128)}, f32[64,1]{0,1:T(1,128)S(1)}, f32[128]{0:T(128)S(1)}, /*index=5*/f32[128]{0:T(128)S(1)}, f32[64,128,2]{1,2,0:T(2,128)S(1)}, s32[]{:T(128)}, s32[]{:T(128)}) while((s32[]{:T(128)}, f32[128,2]{0,1:T(2,128)S(1)}, s32[]{:T(128)}, f32[64,1]{0,1:T(1,128)S(1)}, ...), condition=%wide.region_3.4_spmd.clone, body=%wide.region_2.3_spmd.clone.sunk | while | flops 2436 | bytes 9350 | solution.py:24
  280.4 0.7 fusion.134
  281.9 0.7 fusion.134
  283.3 0.7 fusion.134
  284.8 0.7 fusion.134
  286.2 0.7 fusion.134
  287.7 0.7 fusion.134
  289.2 0.7 fusion.134
  290.6 0.7 fusion.134
  292.1 0.7 fusion.134
  293.5 0.7 fusion.134
  295.0 0.7 fusion.134
  296.4 0.7 fusion.134
  297.9 0.7 fusion.134
  299.4 0.7 fusion.134
  300.8 0.7 fusion.134
  302.3 0.7 fusion.134
  303.7 0.7 fusion.134
  305.2 0.7 fusion.134
  306.6 0.7 fusion.134
  308.1 0.7 fusion.134
  309.6 0.7 fusion.134
  311.0 0.7 fusion.134
  312.5 0.7 fusion.134
  313.9 0.7 fusion.134
  315.4 0.7 fusion.134
  316.8 0.7 fusion.134
  318.3 0.7 fusion.134
  319.8 0.7 fusion.134
  321.2 0.7 fusion.134
  322.7 0.7 fusion.134
  324.1 0.7 fusion.134
  325.6 0.7 fusion.134
  327.0 0.7 fusion.134
  328.5 0.7 fusion.134
  329.9 0.7 fusion.134
  331.4 0.7 fusion.134
  332.9 0.7 fusion.134
  334.3 0.7 fusion.134
  335.8 0.7 fusion.134
  343.1 0.7 fusion.134
  356.2 0.7 fusion.134
  370.7 0.7 fusion.134
  373.0 81.7 %all-gather.1 = f32[8192,2]{0,1:T(2,128)S(1)} all-gather(f32[128,2]{0,1:T(2,128)S(1)} %maximum_add_fusion.2), channel_id=3, replica_groups=mesh['tm'=64,'tile'=8] {'tm'}, dimensions={0}, use_global_device_ids=true | all-gather | bytes 66560 | tf_op jit(solution)/shard_map/all_gather | solution.py:13
  454.7 92.8 %while.21 = (s32[]{:T(128)}, f32[128,2]{0,1:T(2,128)S(1)}, s32[]{:T(128)}, f32[64,1]{0,1:T(1,128)S(1)}, f32[128]{0:T(128)S(1)}, /*index=5*/f32[128]{0:T(128)S(1)...) while((s32[]{:T(128)}, f32[128,2]{0,1:T(2,128)S(1)}, ...), condition=%wide.region_5.6_spmd.clone, body=%wide.region_4.5_spmd.clone.sunk | while | flops 2440 | bytes 9412 | solution.py:24
  547.8 1.4 fusion.98
  (521 shorter events, 153.8 us)
Async XLA Ops:
  0.0 167.9 %copy-start = (bf16[2,16,128,256]{3,2,1,0:T(8,128)(2,1)S(1)}, bf16[2,16,128,256]{3,2,1,0:T(8,128)(2,1)}, u32[]{:S(2)}) copy-start(bf16[2,16,128,256]{3,2,1,0:T(8,128)(2,1)} %param.19) | copy-start | bytes 6291460
  7.0 5.4 copy-start.8
  12.4 3.8 copy-start.4
  12.4 3.8 copy-start.5
  12.9 6.6 %copy-start.7 = (bf16[3,128,128]{2,1,0:T(8,128)(2,1)S(1)}, bf16[3,128,128]{2,1,0:T(8,128)(2,1)}, u32[]{:S(2)}) copy-start(bf16[3,128,128]{2,1,0:T(8,128)(2,1)} %param.18) | copy-start | bytes 294916
  13.0 3.3 collective-permute-start
  14.8 4.5 collective-permute-start.1
  19.5 7.3 %copy-start.6 = (f32[128]{0:T(128)S(1)}, f32[128]{0:T(128)}, u32[]{:S(2)}) copy-start(f32[128]{0:T(128)} %param.24) | copy-start | bytes 1540
  21.0 5.9 %collective-permute-start.2 = (bf16[1,128,1,128]{3,1,2,0:T(8,128)(2,1)S(1)}, bf16[1,128,1,128]{3,1,2,0:T(8,128)(2,1)S(1)}, u32[]{:S(2)}, u32[]{:S(2)}) collective-permute-start(bf16[1,128,1,128]{3,1,2,0:T(8,128)(2,1)S(1)} %get-tuple-element.515), channel_id=1, source_target_pairs={{0,1},{1,2},{2,3},{3,4},{4,5},{5,6},{6,7},{8,9},{9,10},{10,11},{11... | collective-permute-start | bytes 98312 | tf_op jit(solution)/shard_map/ppermute | solution.py:34
  25.5 3.1 collective-permute-start.3
  28.8 6.9 %copy-start.2 = (f32[128]{0:T(128)S(1)}, f32[128]{0:T(128)}, u32[]{:S(2)}) copy-start(f32[128]{0:T(128)} %param.21) | copy-start | bytes 1540
  28.8 6.9 %copy-start.3 = (f32[128]{0:T(128)S(1)}, f32[128]{0:T(128)}, u32[]{:S(2)}) copy-start(f32[128]{0:T(128)} %param.23) | copy-start | bytes 1540
  28.8 6.9 %copy-start.1 = (f32[256,256]{1,0:T(8,128)S(1)}, f32[256,256]{1,0:T(8,128)}, u32[]{:S(2)}) copy-start(f32[256,256]{1,0:T(8,128)} %param.20) | copy-start | bytes 786436
  30.3 135.8 %collective-permute-start.4 = (bf16[1,128,1,128]{3,1,2,0:T(8,128)(2,1)S(1)}, bf16[1,128,1,128]{3,1,2,0:T(8,128)(2,1)S(1)}, u32[]{:S(2)}, u32[]{:S(2)}) collective-permute-start(bf16[1,128,1,128]{3,1,2,0:T(8,128)(2,1)S(1)} %get-tuple-element.513), channel_id=1, source_target_pairs={{0,1},{1,2},{2,3},{3,4},{4,5},{5,6},{6,7},{8,9},{9,10},{10,11},{11... | collective-permute-start | bytes 98312 | tf_op jit(solution)/shard_map/ppermute | solution.py:34
  34.4 131.7 %collective-permute-start.5 = (bf16[1,128,1,128]{3,1,2,0:T(8,128)(2,1)S(1)}, bf16[1,128,1,128]{3,1,2,0:T(8,128)(2,1)S(1)}, u32[]{:S(2)}, u32[]{:S(2)}) collective-permute-start(bf16[1,128,1,128]{3,1,2,0:T(8,128)(2,1)S(1)} %get-tuple-element.514), channel_id=1, source_target_pairs={{1,0},{2,1},{3,2},{4,3},{5,4},{6,5},{7,6},{9,8},{10,9},{11,10},{12... | collective-permute-start | bytes 98312 | tf_op jit(solution)/shard_map/ppermute | solution.py:35
where the time goes:
time: 551 us; the launch traced here: 549 us
  blocking collectives  321 us (58%)
  local copies, waits for them, and re-layouts  100 us (18%)
  other arithmetic  98.2 us (18%)
  starting transfers between devices  14.3 us (3%)
  matrix products  6.68 us (1%)
    all_gather x2, blocking collectives, entering(): everything = jax.tree.map(lambda part: lax.all_gather(part, axis), x)  180 us
    unnamed x1, blocking collectives  128 us
    mul x128, other arithmetic, rotate(): magnitude * (cosine * real_part - sine * imag_part)  94 us
    dynamic_slice x128, local copies, waits for them, and re-layouts, turn(): new = combine(before, jax.tree.map(lambda part: part[at], everything))  84.9 us
    psum x1, blocking collectives, shards(): observed = lax.psum(partial_value, 'tile')  12.8 us
  transfers between devices with their start and end apart: 6, of which 2 were waited for; matrix products, arithmetic and copies ran while one was open for 0% of the time, Pallas kernels for 0%

commit v1 on v0

v1 whole, which is shorter than its diff:
```python
import jax
import jax.numpy as jnp
from jax import lax
from jax.experimental import pallas as pl
from jax.experimental.pallas import tpu as pltpu
from jax.sharding import PartitionSpec as P

PATCH = 8
POOL = 8
LAYERS = 3


def with_halo(x, sides, width):
    for axis, dim in sides:
        size, length = (lax.axis_size(axis), x.shape[dim])
        up = [(i, (i + 1) % size) for i in range(size - 1)]
        down = [(j, i) for i, j in up]
        last = lax.slice_in_dim(x, length - width, length, axis=dim)
        initial = lax.slice_in_dim(x, 0, width, axis=dim)
        before = lax.ppermute(last, axis, up)
        after = lax.ppermute(initial, axis, down)
        x = jnp.concatenate([before, x, after], axis=dim)
    return x


HIGHEST = lax.Precision.HIGHEST


def dot_t(a, b):
    return lax.dot_general(
        a, b, (((1,), (1,)), ((), ())), precision=HIGHEST, preferred_element_type=jnp.float32
    )


def scan_rows(real, imag, mult_real, mult_imag, backward):
    rows = real.shape[0]
    row = lax.broadcasted_iota(jnp.int32, real.shape, 0)
    step = 1
    while step < rows:
        shift = rows - step if backward else step
        kept = row < rows - step if backward else row >= step
        moved_real = jnp.where(kept, pltpu.roll(real, shift, 0), 0.0)
        moved_imag = jnp.where(kept, pltpu.roll(imag, shift, 0), 0.0)
        real, imag = (
            real + mult_real * moved_real - mult_imag * moved_imag,
            imag + mult_imag * moved_real + mult_real * moved_imag,
        )
        mult_real, mult_imag = (
            mult_real * mult_real - mult_imag * mult_imag,
            2.0 * mult_real * mult_imag,
        )
        step *= 2
    return real, imag


def filter_kernel(frame_ref, seen_ref, input_ref, decay_ref, angle_ref, back_decay_ref, back_angle_ref,
                  readout_ref, out_ref):
    modes = decay_ref.shape[1]
    parts = input_ref.shape[1] // seen_ref.shape[1]
    frames = seen_ref.shape[0] // parts
    lanes = seen_ref.shape[1]
    decay, angle = decay_ref[...], angle_ref[...]
    back_decay, back_angle = back_decay_ref[...], back_angle_ref[...]
    gain = jnp.sqrt(1.0 - decay * decay)
    back_gain = jnp.sqrt(1.0 - back_decay * back_decay)
    mode = lax.broadcasted_iota(jnp.int32, (modes, 2 * modes), 0)
    place = lax.broadcasted_iota(jnp.int32, (modes, 2 * modes), 1)
    real_place = (place == 2 * mode).astype(jnp.float32)
    imag_place = (place == 2 * mode + 1).astype(jnp.float32)
    drive = sum(
        dot_t(seen_ref[pl.ds(k, frames, stride=parts), :], input_ref[:, k * lanes : (k + 1) * lanes])
        for k in range(parts)
    )
    real = dot_t(drive, real_place) * gain
    imag = dot_t(drive, imag_place) * gain
    real, imag = scan_rows(real, imag, decay * jnp.cos(angle), decay * jnp.sin(angle), False)
    real, imag = scan_rows(
        real * back_gain,
        imag * back_gain,
        back_decay * jnp.cos(back_angle),
        back_decay * jnp.sin(back_angle),
        True,
    )
    mine = lax.broadcasted_iota(jnp.int32, real.shape, 0) == frame_ref[0]
    real = jnp.sum(jnp.where(mine, real, 0.0), axis=0, keepdims=True)
    imag = jnp.sum(jnp.where(mine, imag, 0.0), axis=0, keepdims=True)
    shares = out_ref.shape[0]
    width = out_ref.shape[1]
    real = jnp.broadcast_to(real, (shares, modes))
    imag = jnp.broadcast_to(imag, (shares, modes))
    laid = jnp.dot(
        real, real_place, precision=HIGHEST
    ) + jnp.dot(imag, imag_place, precision=HIGHEST)
    latent = dot_t(laid, readout_ref[...])
    share = lax.broadcasted_iota(jnp.int32, (shares, width), 0)
    out = latent[:, :width]
    for k in range(1, shares):
        out = jnp.where(share == k, latent[:, k * width : (k + 1) * width], out)
    out_ref[...] = out


def filter_frames(frame, seen, input_map, mode_decay, mode_angle, smooth_decay, smooth_angle, readout, shares):
    vmem = pl.BlockSpec(memory_space=pltpu.VMEM)
    width = readout.shape[0] // shares
    return pl.pallas_call(
        filter_kernel,
        out_shape=jax.ShapeDtypeStruct((shares, width), jnp.float32),
        in_specs=[pl.BlockSpec(memory_space=pltpu.SMEM)] + [vmem] * 7,
        out_specs=vmem,
        name="filter_frames",
    )(
        frame,
        seen,
        input_map,
        mode_decay[None],
        mode_angle[None],
        smooth_decay[None],
        smooth_angle[None],
        readout,
    )


def embed(frames, patch_weight):
    frame_count, height, width = frames.shape
    grid_rows = height // PATCH
    grid_cols = width // PATCH
    patches = (
        frames.reshape(frame_count, grid_rows, PATCH, grid_cols, PATCH)
        .transpose(0, 1, 3, 2, 4)
        .reshape(frame_count, grid_rows, grid_cols, PATCH * PATCH)
    )
    return jax.nn.gelu(jnp.dot(patches, patch_weight, preferred_element_type=jnp.float32)).astype(
        jnp.bfloat16
    )


def conv_layer(hidden, padded, depth_weight, point_weight, layer_index):
    grid_rows = hidden.shape[1]
    grid_cols = hidden.shape[2]
    summed = jnp.zeros(hidden.shape, jnp.float32)
    for row_shift in range(3):
        for col_shift in range(3):
            kernel = depth_weight[layer_index, row_shift, col_shift].astype(jnp.float32)
            summed = (
                summed
                + padded[
                    :, row_shift : row_shift + grid_rows, col_shift : col_shift + grid_cols
                ].astype(jnp.float32)
                * kernel
            )
    depthwise = summed.astype(jnp.bfloat16)
    branch = jax.nn.gelu(
        jnp.dot(depthwise, point_weight[layer_index], preferred_element_type=jnp.float32)
    )
    return (hidden.astype(jnp.float32) + branch).astype(jnp.bfloat16)


def shards(
    movie_frames,
    patch_weight,
    depth_weight,
    point_weight,
    observe_weight,
    input_map,
    mode_decay,
    mode_angle,
    smooth_decay,
    smooth_angle,
    readout,
):
    frame_count, height, width = movie_frames.shape
    grid_rows = height // PATCH
    grid_cols = width // PATCH
    channels = patch_weight.shape[1]
    tile_count = lax.axis_size("tile")
    hidden = embed(movie_frames, patch_weight)
    for layer_index in range(LAYERS):
        widened = with_halo(hidden, (("tile", 2),), 1)
        padded = jnp.pad(widened, ((0, 0), (1, 1), (0, 0), (0, 0)))
        hidden = conv_layer(hidden, padded, depth_weight, point_weight, layer_index)
    pooled = jnp.mean(
        hidden.astype(jnp.float32).reshape(
            frame_count, grid_rows // POOL, POOL, grid_cols // POOL, POOL, channels
        ),
        axis=(2, 4),
    ).astype(jnp.bfloat16)
    features = pooled.transpose(0, 2, 1, 3).reshape(frame_count, -1)
    partial_value = jnp.dot(
        features,
        observe_weight.reshape(-1, observe_weight.shape[-1]),
        preferred_element_type=jnp.float32,
    )
    frames = lax.axis_size("tm")
    seen = lax.all_to_all(
        jnp.broadcast_to(partial_value.reshape(1, -1, 128), (frames, partial_value.shape[1] // 128, 128)),
        "tm",
        0,
        0,
    ).reshape(-1, 128)
    frame = lax.axis_index("tm").astype(jnp.int32)[None]
    shares = filter_frames(
        frame, seen, input_map, mode_decay, mode_angle, smooth_decay, smooth_angle, readout, tile_count
    )
    terms = lax.all_to_all(shares, "tile", 0, 0)
    return jnp.sum(terms, axis=0, keepdims=True)


def solution(mesh):
    placed = (
        P("tm", None, "tile"),
        P(),
        P(),
        P(),
        P("tile", None, None, None),
        P(),
        P(),
        P(),
        P(),
        P(),
        P(),
    )
    return jax.shard_map(
        shards, mesh=mesh, in_specs=placed, out_specs=P("tm", "tile"), check_vma=False
    )
```

time: 551 us -> 90.2 us (0.16)
  the two profiles are of different devices: /device:TPU:4 before, /device:TPU:1 now
where the time goes in v1:
time: 90.2 us; the launch traced here: 89.7 us
  starting transfers between devices  37 us (41%)
  waiting for transfers between devices  16.8 us (19%)
  local copies, waits for them, and re-layouts  13.5 us (15%)
  blocking collectives  11.6 us (13%)
  matrix products  5.26 us (6%)
  Pallas kernels  4.11 us (5%)
  other arithmetic  1.2 us (1%)
    all_to_all x1, starting transfers between devices, shards(): lax.all_to_all(jnp.broadcast_to(partial_value.reshape(1, -1, 128), (frame...  14.1 us
    all_to_all x1, waiting for transfers between devices, shards(): lax.all_to_all(jnp.broadcast_to(partial_value.reshape(1, -1, 128), (frame...  13.7 us
    ppermute x3, starting transfers between devices, with_halo(): after = lax.ppermute(initial, axis, down)  12.9 us
    all_to_all x1, blocking collectives, shards(): terms = lax.all_to_all(shares, 'tile', 0, 0)  11.6 us
    ppermute x3, starting transfers between devices, with_halo(): before = lax.ppermute(last, axis, up)  10 us
    reshape x1, local copies, waits for them, and re-layouts, embed(): frames.reshape(frame_count, grid_rows, PATCH, grid_cols, PATCH)  6.83 us
    transpose x1, local copies, waits for them, and re-layouts, embed(): patches = frames.reshape(frame_count, grid_rows, PATCH, grid_cols, PATCH)...  5.35 us
    dot_general x3, matrix products, conv_layer(): jnp.dot(depthwise, point_weight[layer_index], preferred_element_type=jnp....  4.33 us
  transfers between devices with their start and end apart: 7, of which 4 were waited for; matrix products, arithmetic and copies ran while one was open for 0% of the time, Pallas kernels for 0%

profile of v1, /device:TPU:1, one launch (start us, length us, event | category | flops | bytes accessed | tf_op | source)
XLA Modules:
  0.0 89.7 jit_solution(1258607029413236617)
XLA Ops:
  0.0 0.0 copy-start
  0.0 6.8 %reshape.201 = bf16[1,128,8,16,8]{4,3,2,1,0:T(8,128)(2,1)} reshape(bf16[1,1024,128]{2,1,0:T(8,128)(2,1)} %param.11) | data formatting | bytes 524288 | tf_op jit(solution)/shard_map/reshape | solution.py:128
  6.8 5.4 %copy.14 = bf16[1,128,16,8,8]{1,4,3,2,0:T(8,128)(2,1)S(1)} copy(bf16[1,128,16,8,8]{4,2,3,1,0:T(8,128)(2,1)} %bitcast.190) | data formatting | bytes 524288 | tf_op jit(solution)/shard_map/transpose | solution.py:129
  12.2 0.0 copy-done
  12.2 0.0 copy-start.3
  12.2 0.5 fusion.35
  12.8 0.0 copy-start.4
  12.8 8.9 %collective-permute-start.1 = (bf16[1,128,1,128]{3,1,2,0:T(8,128)(2,1)S(1)}, bf16[1,128,1,128]{3,1,2,0:T(8,128)(2,1)S(1)}, u32[]{:S(2)}, u32[]{:S(2)}) collective-permute-start(bf16[1,128,1,128]{3,1,2,0:T(8,128)(2,1)S(1)} %get-tuple-element.10), channel_id=1, source_target_pairs={{1,0},{2,1},{3,2},{4,3},{5,4},{6,5},{7,6},{9,8},{10,9},{11,10},{12... | collective-permute-start | bytes 98312 | tf_op jit(solution)/shard_map/ppermute | solution.py:21
  21.7 1.9 %collective-permute-start = (bf16[1,128,1,128]{3,1,2,0:T(8,128)(2,1)S(1)}, bf16[1,128,1,128]{3,1,2,0:T(8,128)(2,1)S(1)}, u32[]{:S(2)}, u32[]{:S(2)}) collective-permute-start(bf16[1,128,1,128]{3,1,2,0:T(8,128)(2,1)S(1)} %get-tuple-element.9), channel_id=1, source_target_pairs={{0,1},{1,2},{2,3},{3,4},{4,5},{5,6},{6,7},{8,9},{9,10},{10,11},{11... | collective-permute-start | bytes 98312 | tf_op jit(solution)/shard_map/ppermute | solution.py:20
  23.6 0.0 copy-done.3
  23.6 0.0 collective-permute-done.1
  23.7 1.1 %collective-permute-done = bf16[1,128,1,128]{3,1,2,0:T(8,128)(2,1)S(1)} collective-permute-done((bf16[1,128,1,128]{3,1,2,0:T(8,128)(2,1)S(1)}, bf16[1,128,1,128]{3,1,2,0:T(8,128)(2,1)S(1)}, u32[]{:S(2)}, u32[]{:S(2)}) %collective-permute-start) | collective-permute-done | bytes 32800 | tf_op jit(solution)/shard_map/ppermute | solution.py:20
  24.8 0.2 select_maximum_fusion.4
  25.0 0.0 copy-done.4
  25.0 1.4 %fusion.11 = bf16[128,16,128]{2,0,1:T(8,128)(2,1)S(1)} fusion(bf16[128,16,128]{2,0,1:T(8,128)(2,1)S(1)} %fusion.35, bf16[1,130,18,128]{3,1,2,0:T(8,128)(2,1)S(1)} %select_maximum_fusion.4, bf16[1,128,1,128]{3,1,2,0:T(8,128)(2,1)S(1)} %collective-permute-done.1, bf16[1,128,16,128]{3,1,2,0:T(8,128)(2,1)S(1)} %bitcast.194, ...), kind=kOutput, calls=%fused_computation.23 | convolution fusion | flops 77594624 | bytes 5345792 | tf_op jit(solution)/shard_map/dot_general | solution.py:153
  26.4 2.1 %collective-permute-start.3 = (bf16[1,128,1,128]{3,1,2,0:T(8,128)(2,1)S(1)}, bf16[1,128,1,128]{3,1,2,0:T(8,128)(2,1)S(1)}, u32[]{:S(2)}, u32[]{:S(2)}) collective-permute-start(bf16[1,128,1,128]{3,1,2,0:T(8,128)(2,1)S(1)} %get-tuple-element.8), channel_id=1, source_target_pairs={{1,0},{2,1},{3,2},{4,3},{5,4},{6,5},{7,6},{9,8},{10,9},{11,10},{12... | collective-permute-start | bytes 98312 | tf_op jit(solution)/shard_map/ppermute | solution.py:21
  28.5 3.9 %collective-permute-start.2 = (bf16[1,128,1,128]{3,1,2,0:T(8,128)(2,1)S(1)}, bf16[1,128,1,128]{3,1,2,0:T(8,128)(2,1)S(1)}, u32[]{:S(2)}, u32[]{:S(2)}) collective-permute-start(bf16[1,128,1,128]{3,1,2,0:T(8,128)(2,1)S(1)} %get-tuple-element.7), channel_id=1, source_target_pairs={{0,1},{1,2},{2,3},{3,4},{4,5},{5,6},{6,7},{8,9},{9,10},{10,11},{11... | collective-permute-start | bytes 98312 | tf_op jit(solution)/shard_map/ppermute | solution.py:20
  32.4 0.0 collective-permute-done.3
  32.4 1.0 %collective-permute-done.2 = bf16[1,128,1,128]{3,1,2,0:T(8,128)(2,1)S(1)} collective-permute-done((bf16[1,128,1,128]{3,1,2,0:T(8,128)(2,1)S(1)}, bf16[1,128,1,128]{3,1,2,0:T(8,128)(2,1)S(1)}, u32[]{:S(2)}, u32[]{:S(2)}) %collective-permute-start.2) | collective-permute-done | bytes 32800 | tf_op jit(solution)/shard_map/ppermute | solution.py:20
  33.4 0.2 select_maximum_fusion.2
  33.6 1.4 %fusion.19 = bf16[128,16,128]{2,0,1:T(8,128)(2,1)S(1)} fusion(bf16[128,16,128]{2,0,1:T(8,128)(2,1)S(1)} %fusion.11, bf16[1,130,18,128]{3,1,2,0:T(8,128)(2,1)S(1)} %select_maximum_fusion.2, bf16[1,128,1,128]{3,1,2,0:T(8,128)(2,1)S(1)} %collective-permute-done.3, bf16[1,128,16,128]{3,1,2,0:T(8,128)(2,1)S(1)} %bitcast.200, ...), kind=kOutput, calls=%fused_computation.31 | convolution fusion | flops 77594624 | bytes 5345792 | tf_op jit(solution)/shard_map/dot_general | solution.py:153
  35.1 1.9 %collective-permute-start.5 = (bf16[1,128,1,128]{3,1,2,0:T(8,128)(2,1)S(1)}, bf16[1,128,1,128]{3,1,2,0:T(8,128)(2,1)S(1)}, u32[]{:S(2)}, u32[]{:S(2)}) collective-permute-start(bf16[1,128,1,128]{3,1,2,0:T(8,128)(2,1)S(1)} %get-tuple-element.6), channel_id=1, source_target_pairs={{1,0},{2,1},{3,2},{4,3},{5,4},{6,5},{7,6},{9,8},{10,9},{11,10},{12... | collective-permute-start | bytes 98312 | tf_op jit(solution)/shard_map/ppermute | solution.py:21
  37.0 4.2 %collective-permute-start.4 = (bf16[1,128,1,128]{3,1,2,0:T(8,128)(2,1)S(1)}, bf16[1,128,1,128]{3,1,2,0:T(8,128)(2,1)S(1)}, u32[]{:S(2)}, u32[]{:S(2)}) collective-permute-start(bf16[1,128,1,128]{3,1,2,0:T(8,128)(2,1)S(1)} %get-tuple-element.5), channel_id=1, source_target_pairs={{0,1},{1,2},{2,3},{3,4},{4,5},{5,6},{6,7},{8,9},{9,10},{10,11},{11... | collective-permute-start | bytes 98312 | tf_op jit(solution)/shard_map/ppermute | solution.py:20
  41.2 0.0 collective-permute-done.5
  41.2 1.0 %collective-permute-done.4 = bf16[1,128,1,128]{3,1,2,0:T(8,128)(2,1)S(1)} collective-permute-done((bf16[1,128,1,128]{3,1,2,0:T(8,128)(2,1)S(1)}, bf16[1,128,1,128]{3,1,2,0:T(8,128)(2,1)S(1)}, u32[]{:S(2)}, u32[]{:S(2)}) %collective-permute-start.4) | collective-permute-done | bytes 32800 | tf_op jit(solution)/shard_map/ppermute | solution.py:20
  42.2 0.2 select_maximum_fusion
  42.4 0.0 copy-start.1
  42.4 1.4 %fusion.27 = bf16[128,16,128]{2,0,1:T(8,128)(2,1)S(1)} fusion(bf16[128,16,128]{2,0,1:T(8,128)(2,1)S(1)} %fusion.19, bf16[1,130,18,128]{3,1,2,0:T(8,128)(2,1)S(1)} %select_maximum_fusion, bf16[1,128,1,128]{3,1,2,0:T(8,128)(2,1)S(1)} %collective-permute-done.5, bf16[1,128,16,128]{3,1,2,0:T(8,128)(2,1)S(1)} %bitcast.197, ...), kind=kOutput, calls=%fused_computation.39 | convolution fusion | flops 77594624 | bytes 5345792 | tf_op jit(solution)/shard_map/dot_general | solution.py:153
  43.9 0.1 convert_reduce_fusion
  44.0 0.0 copy-done.1
  44.0 0.4 fusion
  44.4 0.7 broadcast_in_dim.15
  45.1 14.1 %all-to-all-start = ((f32[64,2,128]{2,1,0:T(2,128)}), f32[64,2,128]{2,1,0:T(2,128)S(1)}, u32[]{:S(2)}, u32[]{:S(2)}) async-start(f32[64,2,128]{2,1,0:T(2,128)} %broadcast_in_dim.15), calls=%async_computation | async-start | bytes 131072 | tf_op jit(solution)/shard_map/all_to_all | solution.py:194
  59.2 13.7 %all-to-all-done = f32[64,2,128]{2,1,0:T(2,128)S(1)} async-done(((f32[64,2,128]{2,1,0:T(2,128)}), f32[64,2,128]{2,1,0:T(2,128)S(1)}, u32[]{:S(2)}, u32[]{:S(2)}) %all-to-all-start) | async-done | bytes 65568 | tf_op jit(solution)/shard_map/all_to_all | solution.py:194
  72.9 0.0 copy-start.2
  72.9 0.6 copy-done.2
  73.5 4.1 %filter_frames.1 = f32[8,32]{1,0:T(8,128)} custom-call(s32[1]{0:T(128)} %bitcast.frame_ref, f32[128,128]{1,0:T(8,128)} %bitcast.202, f32[256,256]{1,0:T(8,128)} %input_ref.1, f32[1,128]{1,0:T(1,128)} %bitcast.206, f32[1,128]{1,0:T(1,128)} %bitcast.207, f32[1,128]{1,0:T(1,128)} %bitcast.208, f32[1,128]{1,0:T(1,128)} %bitcast.209, f32[256,256]{1,0:T(8,128)} %readout_ref.1), custom_call_target="tpu_custom_call" | custom-call | tf_op jit(solution)/shard_map/filter_frames/pallas_call | solution.py:105
  77.6 11.6 %all_to_all.14 = f32[8,1,32]{2,1,0:T(1,128)S(1)} all-to-all(f32[8,1,32]{2,1,0:T(1,128)} %bitcast.204), channel_id=1, replica_groups=mesh['tm'=64,'tile'=8] {'tile'}, dimensions={0} | all-to-all | bytes 2048 | tf_op jit(solution)/shard_map/all_to_all | solution.py:204
  89.2 0.5 reduce_sum.19
  (7 shorter events, 0.1 us)
Async XLA Ops:
  0.0 12.2 %copy-start = (bf16[64,128]{1,0:T(8,128)(2,1)S(1)}, bf16[64,128]{1,0:T(8,128)(2,1)}, u32[]{:S(2)}) copy-start(bf16[64,128]{1,0:T(8,128)(2,1)} %param.12) | copy-start | bytes 49156
  12.2 11.4 %copy-start.3 = (bf16[3,3,3,128]{3,2,1,0:T(4,128)(2,1)S(1)}, bf16[3,3,3,128]{3,2,1,0:T(4,128)(2,1)}, u32[]{:S(2)}) copy-start(bf16[3,3,3,128]{3,2,1,0:T(4,128)(2,1)} %param.13) | copy-start | bytes 20740
  12.8 12.2 %copy-start.4 = (bf16[3,128,128]{2,1,0:T(8,128)(2,1)S(1)}, bf16[3,128,128]{2,1,0:T(8,128)(2,1)}, u32[]{:S(2)}) copy-start(bf16[3,128,128]{2,1,0:T(8,128)(2,1)} %param.14) | copy-start | bytes 294916
  12.8 10.9 %collective-permute-start.1 = (bf16[1,128,1,128]{3,1,2,0:T(8,128)(2,1)S(1)}, bf16[1,128,1,128]{3,1,2,0:T(8,128)(2,1)S(1)}, u32[]{:S(2)}, u32[]{:S(2)}) collective-permute-start(bf16[1,128,1,128]{3,1,2,0:T(8,128)(2,1)S(1)} %get-tuple-element.10), channel_id=1, source_target_pairs={{1,0},{2,1},{3,2},{4,3},{5,4},{6,5},{7,6},{9,8},{10,9},{11,10},{12... | collective-permute-start | bytes 98312 | tf_op jit(solution)/shard_map/ppermute | solution.py:21
  21.7 3.1 %collective-permute-start = (bf16[1,128,1,128]{3,1,2,0:T(8,128)(2,1)S(1)}, bf16[1,128,1,128]{3,1,2,0:T(8,128)(2,1)S(1)}, u32[]{:S(2)}, u32[]{:S(2)}) collective-permute-start(bf16[1,128,1,128]{3,1,2,0:T(8,128)(2,1)S(1)} %get-tuple-element.9), channel_id=1, source_target_pairs={{0,1},{1,2},{2,3},{3,4},{4,5},{5,6},{6,7},{8,9},{9,10},{10,11},{11... | collective-permute-start | bytes 98312 | tf_op jit(solution)/shard_map/ppermute | solution.py:20
  26.4 6.0 %collective-permute-start.3 = (bf16[1,128,1,128]{3,1,2,0:T(8,128)(2,1)S(1)}, bf16[1,128,1,128]{3,1,2,0:T(8,128)(2,1)S(1)}, u32[]{:S(2)}, u32[]{:S(2)}) collective-permute-start(bf16[1,128,1,128]{3,1,2,0:T(8,128)(2,1)S(1)} %get-tuple-element.8), channel_id=1, source_target_pairs={{1,0},{2,1},{3,2},{4,3},{5,4},{6,5},{7,6},{9,8},{10,9},{11,10},{12... | collective-permute-start | bytes 98312 | tf_op jit(solution)/shard_map/ppermute | solution.py:21
  28.5 4.9 %collective-permute-start.2 = (bf16[1,128,1,128]{3,1,2,0:T(8,128)(2,1)S(1)}, bf16[1,128,1,128]{3,1,2,0:T(8,128)(2,1)S(1)}, u32[]{:S(2)}, u32[]{:S(2)}) collective-permute-start(bf16[1,128,1,128]{3,1,2,0:T(8,128)(2,1)S(1)} %get-tuple-element.7), channel_id=1, source_target_pairs={{0,1},{1,2},{2,3},{3,4},{4,5},{5,6},{6,7},{8,9},{9,10},{10,11},{11... | collective-permute-start | bytes 98312 | tf_op jit(solution)/shard_map/ppermute | solution.py:20
  35.1 6.2 %collective-permute-start.5 = (bf16[1,128,1,128]{3,1,2,0:T(8,128)(2,1)S(1)}, bf16[1,128,1,128]{3,1,2,0:T(8,128)(2,1)S(1)}, u32[]{:S(2)}, u32[]{:S(2)}) collective-permute-start(bf16[1,128,1,128]{3,1,2,0:T(8,128)(2,1)S(1)} %get-tuple-element.6), channel_id=1, source_target_pairs={{1,0},{2,1},{3,2},{4,3},{5,4},{6,5},{7,6},{9,8},{10,9},{11,10},{12... | collective-permute-start | bytes 98312 | tf_op jit(solution)/shard_map/ppermute | solution.py:21
  37.0 5.2 %collective-permute-start.4 = (bf16[1,128,1,128]{3,1,2,0:T(8,128)(2,1)S(1)}, bf16[1,128,1,128]{3,1,2,0:T(8,128)(2,1)S(1)}, u32[]{:S(2)}, u32[]{:S(2)}) collective-permute-start(bf16[1,128,1,128]{3,1,2,0:T(8,128)(2,1)S(1)} %get-tuple-element.5), channel_id=1, source_target_pairs={{0,1},{1,2},{2,3},{3,4},{4,5},{5,6},{6,7},{8,9},{9,10},{10,11},{11... | collective-permute-start | bytes 98312 | tf_op jit(solution)/shard_map/ppermute | solution.py:20
  42.4 1.6 %copy-start.1 = (bf16[2,16,128,256]{3,2,1,0:T(8,128)(2,1)S(1)}, bf16[2,16,128,256]{3,2,1,0:T(8,128)(2,1)}, u32[]{:S(2)}) copy-start(bf16[2,16,128,256]{3,2,1,0:T(8,128)(2,1)} %param.15) | copy-start | bytes 6291460
  45.1 27.8 %all-to-all-start = ((f32[64,2,128]{2,1,0:T(2,128)}), f32[64,2,128]{2,1,0:T(2,128)S(1)}, u32[]{:S(2)}, u32[]{:S(2)}) async-start(f32[64,2,128]{2,1,0:T(2,128)} %broadcast_in_dim.15), calls=%async_computation | async-start | bytes 131072 | tf_op jit(solution)/shard_map/all_to_all | solution.py:194
  72.9 0.6 copy-start.2

commit v2 on v1

--- a/solution.py
+++ b/solution.py
@@ -10,17 +10,183 @@
 LAYERS = 3
 
 
-def with_halo(x, sides, width):
-    for axis, dim in sides:
-        size, length = (lax.axis_size(axis), x.shape[dim])
-        up = [(i, (i + 1) % size) for i in range(size - 1)]
-        down = [(j, i) for i, j in up]
-        last = lax.slice_in_dim(x, length - width, length, axis=dim)
-        initial = lax.slice_in_dim(x, 0, width, axis=dim)
-        before = lax.ppermute(last, axis, up)
-        after = lax.ppermute(initial, axis, down)
-        x = jnp.concatenate([before, x, after], axis=dim)
-    return x
+PAD = 8
+EDGE = LAYERS
+VMEM = pl.BlockSpec(memory_space=pltpu.VMEM)
+CUBIC = 0.044715
+ROOT = 0.7978845608028654
+
+
+def gelu_of_half(y):
+    return y + y * jnp.tanh(y * (2.0 * ROOT + (8.0 * ROOT * CUBIC) * (y * y)))
+
+
+def put_column(ref, at, value):
+    rows, lanes = value.shape
+    zeros = jnp.zeros((PAD, lanes), ref.dtype)
+    ref[at, :PAD, :] = zeros
+    ref[at, PAD : PAD + rows, :] = value.astype(ref.dtype)
+    ref[at, PAD + rows :, :] = zeros
+
+
+def embed_kernel(frame_ref, weight_ref, hidden_ref, first_ref, last_ref, wide_ref, spread_ref):
+    lanes = frame_ref.shape[2]
+    rows = frame_ref.shape[1] // PATCH
+    channels = weight_ref.shape[1]
+    group = 32
+    cells = group // PATCH
+    columns = lanes // PATCH
+    wide_ref[...] = frame_ref[0].astype(jnp.float32)
+    weight = weight_ref[...].astype(jnp.float32) * 0.5
+    spread_ref[...] = jnp.zeros(spread_ref.shape, spread_ref.dtype)
+    for i in range(PATCH):
+        for c in range(cells):
+            at = (i * cells + c) * PATCH
+            spread_ref[at : at + PATCH, c * channels : (c + 1) * channels] = weight[i * PATCH : (i + 1) * PATCH]
+    spread = spread_ref[...].astype(jnp.bfloat16)
+    lines = [wide_ref[pl.ds(i, rows, stride=PATCH), :] for i in range(PATCH)]
+    lane_group = lax.broadcasted_iota(jnp.int32, (rows, lanes), 1) // group
+    per = lanes // group
+    for q in range(per):
+        halves = []
+        for h in range(PATCH // per):
+            half = None
+            for s in range(per):
+                line = lines[h * per + s]
+                shift = ((s - q) * group) % lanes
+                line = pltpu.roll(line, shift, 1) if shift else line
+                half = line if half is None else jnp.where(lane_group == s, line, half)
+            halves.append(half.astype(jnp.bfloat16))
+        y = jnp.dot(jnp.concatenate(halves, axis=1), spread, preferred_element_type=jnp.float32)
+        for c in range(cells):
+            value = gelu_of_half(y[:, c * channels : (c + 1) * channels]).astype(jnp.bfloat16)
+            at = q * cells + c
+            put_column(hidden_ref, at, value)
+            if at < EDGE:
+                first_ref[at] = value
+            if at >= columns - EDGE:
+                last_ref[at - (columns - EDGE)] = value
+
+
+def embed(frames, patch_weight):
+    _, height, lanes = frames.shape
+    rows, columns, channels = height // PATCH, lanes // PATCH, patch_weight.shape[1]
+    edge = jax.ShapeDtypeStruct((EDGE, rows, channels), jnp.bfloat16)
+    return pl.pallas_call(
+        embed_kernel,
+        out_shape=(jax.ShapeDtypeStruct((columns, rows + 2 * PAD, channels), jnp.float32), edge, edge),
+        in_specs=[VMEM] * 2,
+        out_specs=(VMEM,) * 3,
+        scratch_shapes=[
+            pltpu.VMEM((height, lanes), jnp.float32),
+            pltpu.VMEM((256, 4 * channels), jnp.float32),
+        ],
+        compiler_params=pltpu.CompilerParams(vmem_limit_bytes=16 << 20),
+        name="embed",
+    )(frames, patch_weight)
+
+
+def taps_of(depth_ref, layer):
+    return [depth_ref[layer, k // 3, k % 3 : k % 3 + 1, :].astype(jnp.float32) for k in range(9)]
+
+
+def new_column(left, middle, right, taps, weight):
+    rows = middle.shape[0] - 2 * PAD
+    total = None
+    for dc, ref in enumerate((left, middle, right)):
+        for dr in range(3):
+            term = ref[PAD - 1 + dr : PAD - 1 + dr + rows, :] * taps[3 * dr + dc]
+            total = term if total is None else total + term
+    y = jnp.dot(total.astype(jnp.bfloat16), weight, preferred_element_type=jnp.float32)
+    return middle[PAD : PAD + rows, :] + gelu_of_half(y)
+
+
+def inner_kernel(hidden_ref, depth_ref, point_ref, one_ref, two_ref, sum_ref):
+    columns = hidden_ref.shape[0]
+    taps = [taps_of(depth_ref, layer) for layer in range(LAYERS)]
+    weights = [(point_ref[layer].astype(jnp.float32) * 0.5).astype(jnp.bfloat16) for layer in range(LAYERS)]
+    for layer, (source, target) in enumerate(((hidden_ref, one_ref), (one_ref, two_ref), (two_ref, None))):
+        for at in range(layer + 1, columns - layer - 1):
+            value = new_column(
+                source.at[at - 1], source.at[at], source.at[at + 1], taps[layer], weights[layer]
+            )
+            if target is not None:
+                put_column(target, at, value)
+            elif at in (EDGE, columns // 2):
+                sum_ref[at // POOL] = value
+            else:
+                sum_ref[at // POOL] += value
+
+
+def outer_kernel(inside_ref, hidden_ref, one_ref, two_ref, sum_ref, first_ref, last_ref, depth_ref, point_ref,
+                 pooled_ref, border_ref):
+    columns = hidden_ref.shape[0]
+    taps = [taps_of(depth_ref, layer) for layer in range(LAYERS)]
+    weights = [(point_ref[layer].astype(jnp.float32) * 0.5).astype(jnp.bfloat16) for layer in range(LAYERS)]
+    inside = (inside_ref[0].astype(jnp.float32), inside_ref[1].astype(jnp.float32))
+    for side in range(2):
+        halo = (first_ref, last_ref)[side]
+        for k in range(EDGE):
+            put_column(border_ref.at[side, 0], k, halo[k].astype(jnp.float32))
+
+    def view(side, level, at):
+        if level <= at < columns - level:
+            return (hidden_ref, one_ref, two_ref)[level].at[at]
+        return border_ref.at[side, level, at + EDGE - level if side == 0 else at - columns + level]
+
+    sums = [sum_ref[0], sum_ref[1]]
+    for layer in range(LAYERS):
+        for side in range(2):
+            for k in range(EDGE):
+                at = k - 2 + layer if side == 0 else columns - 1 - layer + k
+                value = new_column(
+                    view(side, layer, at - 1),
+                    view(side, layer, at),
+                    view(side, layer, at + 1),
+                    taps[layer],
+                    weights[layer],
+                )
+                if layer == LAYERS - 1:
+                    sums[side] = sums[side] + value
+                else:
+                    if at < 0 or at >= columns:
+                        value = value * inside[side]
+                    put_column(border_ref.at[side, layer + 1], k, value)
+    rows = sums[0].shape[0]
+    for g in range(2):
+        pooled_ref[g] = (
+            jnp.sum(sums[g].reshape(rows // POOL, POOL, sums[g].shape[1]), axis=1) * (1.0 / (POOL * POOL))
+        ).astype(jnp.bfloat16)
+
+
+def encode(frames, patch_weight, depth_weight, point_weight):
+    size, here = lax.axis_size("tile"), lax.axis_index("tile")
+    hidden, first, last = embed(frames, patch_weight)
+    up = [(i, i + 1) for i in range(size - 1)]
+    before = lax.ppermute(last, "tile", up)
+    after = lax.ppermute(first, "tile", [(j, i) for i, j in up])
+    columns, padded, channels = hidden.shape
+    rows = padded - 2 * PAD
+    level = jax.ShapeDtypeStruct(hidden.shape, jnp.float32)
+    one, two, total = pl.pallas_call(
+        inner_kernel,
+        out_shape=(level, level, jax.ShapeDtypeStruct((2, rows, channels), jnp.float32)),
+        in_specs=[VMEM] * 3,
+        out_specs=(VMEM,) * 3,
+        compiler_params=pltpu.CompilerParams(vmem_limit_bytes=16 << 20),
+        cost_estimate=pl.CostEstimate(flops=400_000_000, bytes_accessed=4_000_000, transcendentals=0),
+        name="inner",
+    )(hidden, depth_weight, point_weight)
+    inside = jnp.stack([here > 0, here < size - 1]).astype(jnp.int32)
+    return pl.pallas_call(
+        outer_kernel,
+        out_shape=jax.ShapeDtypeStruct((2, rows // POOL, channels), jnp.bfloat16),
+        in_specs=[pl.BlockSpec(memory_space=pltpu.SMEM)] + [VMEM] * 8,
+        out_specs=VMEM,
+        scratch_shapes=[pltpu.VMEM((2, LAYERS, EDGE, padded, channels), jnp.float32)],
+        compiler_params=pltpu.CompilerParams(vmem_limit_bytes=20 << 20),
+        name="outer",
+    )(inside, hidden, one, two, total, before, after, depth_weight, point_weight)
 
 
 HIGHEST = lax.Precision.HIGHEST
@@ -107,6 +273,7 @@
         out_shape=jax.ShapeDtypeStruct((shares, width), jnp.float32),
         in_specs=[pl.BlockSpec(memory_space=pltpu.SMEM)] + [vmem] * 7,
         out_specs=vmem,
+        compiler_params=pltpu.CompilerParams(vmem_limit_bytes=8 << 20),
         name="filter_frames",
     )(
         frame,
@@ -118,41 +285,6 @@
         smooth_angle[None],
         readout,
     )
-
-
-def embed(frames, patch_weight):
-    frame_count, height, width = frames.shape
-    grid_rows = height // PATCH
-    grid_cols = width // PATCH
-    patches = (
-        frames.reshape(frame_count, grid_rows, PATCH, grid_cols, PATCH)
-        .transpose(0, 1, 3, 2, 4)
-        .reshape(frame_count, grid_rows, grid_cols, PATCH * PATCH)
-    )
-    return jax.nn.gelu(jnp.dot(patches, patch_weight, preferred_element_type=jnp.float32)).astype(
-        jnp.bfloat16
-    )
-
-
-def conv_layer(hidden, padded, depth_weight, point_weight, layer_index):
-    grid_rows = hidden.shape[1]
-    grid_cols = hidden.shape[2]
-    summed = jnp.zeros(hidden.shape, jnp.float32)
-    for row_shift in range(3):
-        for col_shift in range(3):
-            kernel = depth_weight[layer_index, row_shift, col_shift].astype(jnp.float32)
-            summed = (
-                summed
-                + padded[
-                    :, row_shift : row_shift + grid_rows, col_shift : col_shift + grid_cols
-                ].astype(jnp.float32)
-                * kernel
-            )
-    depthwise = summed.astype(jnp.bfloat16)
-    branch = jax.nn.gelu(
-        jnp.dot(depthwise, point_weight[layer_index], preferred_element_type=jnp.float32)
-    )
-    return (hidden.astype(jnp.float32) + branch).astype(jnp.bfloat16)
 
 
 def shards(
@@ -168,36 +300,22 @@
     smooth_angle,
     readout,
 ):
-    frame_count, height, width = movie_frames.shape
-    grid_rows = height // PATCH
-    grid_cols = width // PATCH
-    channels = patch_weight.shape[1]
     tile_count = lax.axis_size("tile")
-    hidden = embed(movie_frames, patch_weight)
-    for layer_index in range(LAYERS):
-        widened = with_halo(hidden, (("tile", 2),), 1)
-        padded = jnp.pad(widened, ((0, 0), (1, 1), (0, 0), (0, 0)))
-        hidden = conv_layer(hidden, padded, depth_weight, point_weight, layer_index)
-    pooled = jnp.mean(
-        hidden.astype(jnp.float32).reshape(
-            frame_count, grid_rows // POOL, POOL, grid_cols // POOL, POOL, channels
-        ),
-        axis=(2, 4),
-    ).astype(jnp.bfloat16)
-    features = pooled.transpose(0, 2, 1, 3).reshape(frame_count, -1)
     partial_value = jnp.dot(
-        features,
+        encode(movie_frames, patch_weight, depth_weight, point_weight).reshape(1, -1),
         observe_weight.reshape(-1, observe_weight.shape[-1]),
         preferred_element_type=jnp.float32,
     )
     frames = lax.axis_size("tm")
+    partial_value, frame = lax.optimization_barrier(
+        (partial_value, lax.axis_index("tm").astype(jnp.int32)[None])
+    )
     seen = lax.all_to_all(
         jnp.broadcast_to(partial_value.reshape(1, -1, 128), (frames, partial_value.shape[1] // 128, 128)),
         "tm",
         0,
         0,
     ).reshape(-1, 128)
-    frame = lax.axis_index("tm").astype(jnp.int32)[None]
     shares = filter_frames(
         frame, seen, input_map, mode_decay, mode_angle, smooth_decay, smooth_angle, readout, tile_count
     )

time: 90.2 us -> 63.3 us (0.70)
  blocking collectives: 11.6 us -> 39.1 us
  starting transfers between devices: 37 us -> 10 us
  waiting for transfers between devices: 16.8 us -> 0.01 us
  local copies, waits for them, and re-layouts: 13.5 us -> 5.06 us
  matrix products: 5.26 us -> 0.39 us
  Pallas kernels: 4.11 us -> 7.44 us
    all_to_all x0 -> x1, blocking collectives: none -> 28.5 us  [shards(): lax.all_to_all(jnp.broadcast_to(partial_value.reshape(1, -1, 128), (frame...]
    all_to_all x1 -> x0, starting transfers between devices: 14.1 us -> none  [shards(): lax.all_to_all(jnp.broadcast_to(partial_value.reshape(1, -1, 128), (frame...]
    all_to_all x1 -> x0, waiting for transfers between devices: 13.7 us -> none  [shards(): lax.all_to_all(jnp.broadcast_to(partial_value.reshape(1, -1, 128), (frame...]
    ppermute x6 -> x2, starting transfers between devices: 22.9 us -> 10 us  [the longest x1 5.45 us: encode(): after = lax.ppermute(first, 'tile', [(j, i) for i, j in up])]
    reshape x1 -> x0, local copies, waits for them, and re-layouts: 6.83 us -> none  [embed(): frames.reshape(frame_count, grid_rows, PATCH, grid_cols, PATCH)]
    transpose x1 -> x0, local copies, waits for them, and re-layouts: 5.35 us -> none  [embed(): patches = frames.reshape(frame_count, grid_rows, PATCH, grid_cols, PATCH)...]
    pallas_call x0 -> x3, Pallas kernels: none -> 5.07 us  [the longest x1 2.07 us: encode(): pl.pallas_call(inner_kernel, out_shape=(level, level, jax.ShapeDtypeStruc...]
    dot_general x5 -> x1, matrix products: 5.26 us -> 0.39 us  [shards(): jnp.dot(encode(movie_frames, patch_weight, depth_weight, point_weight).re...]
  transfers between devices with their start and end apart: 7 -> 2, of which waited for: 4 -> 0; matrix products, arithmetic and copies ran while one was open for 0% -> 0% of each run, Pallas kernels for 0% -> 3%
where the time goes in v2:
time: 63.3 us; the launch traced here: 62.8 us
  blocking collectives  39.1 us (62%)
  starting transfers between devices  10 us (16%)
  Pallas kernels  7.44 us (12%)
  local copies, waits for them, and re-layouts  5.06 us (8%)
    all_to_all x1, blocking collectives, shards(): lax.all_to_all(jnp.broadcast_to(partial_value.reshape(1, -1, 128), (frame...  28.5 us
    all_to_all x1, blocking collectives, shards(): terms = lax.all_to_all(shares, 'tile', 0, 0)  10.6 us
    ppermute x1, starting transfers between devices, encode(): after = lax.ppermute(first, 'tile', [(j, i) for i, j in up])  5.45 us
    unnamed x26, local copies, waits for them, and re-layouts  5.04 us
    ppermute x1, starting transfers between devices, encode(): before = lax.ppermute(last, 'tile', up)  4.58 us
    pallas_call x1, Pallas kernels, filter_frames(): pl.pallas_call(filter_kernel, out_shape=jax.ShapeDtypeStruct((shares, wid...  2.36 us
    pallas_call x1, Pallas kernels, encode(): pl.pallas_call(inner_kernel, out_shape=(level, level, jax.ShapeDtypeStruc...  2.07 us
    pallas_call x1, Pallas kernels, encode(): pl.pallas_call(outer_kernel, out_shape=jax.ShapeDtypeStruct((2, rows // P...  1.71 us
  transfers between devices with their start and end apart: 2, of which 0 were waited for; matrix products, arithmetic and copies ran while one was open for 0% of the time, Pallas kernels for 3%

profile of v2, /device:TPU:1, one launch (start us, length us, event | category | flops | bytes accessed | tf_op | source)
XLA Modules:
  0.0 62.8 jit_solution(1567611354931385444)
XLA Ops:
  0.0 0.0 copy-start
  0.0 0.0 copy-start.1
  0.0 1.1 %copy-done.1 = bf16[1,1024,128]{2,1,0:T(8,128)(2,1)S(1)} copy-done((bf16[1,1024,128]{2,1,0:T(8,128)(2,1)S(1)}, bf16[1,1024,128]{2,1,0:T(8,128)(2,1)}, u32[]{:S(2)}) %copy-start.1) | copy-done | bytes 262168
  1.1 0.0 copy-start.6
  1.1 0.7 %copy-done.6 = bf16[64,128]{1,0:T(8,128)(2,1)S(1)} copy-done((bf16[64,128]{1,0:T(8,128)(2,1)S(1)}, bf16[64,128]{1,0:T(8,128)(2,1)}, u32[]{:S(2)}) %copy-start.6) | copy-done | bytes 16408
  1.8 1.3 %embed.1 = (f32[16,144,128]{2,1,0:T(8,128)S(1)}, bf16[3,128,128]{2,1,0:T(8,128)(2,1)}, bf16[3,128,128]{2,1,0:T(8,128)(2,1)}) custom-call(bf16[1,1024,128]{2,1,0:T(8,128)(2,1)S(1)} %copy-done.1, bf16[64,128]{1,0:T(8,128)(2,1)S(1)} %copy-done.6), custom_call_target="tpu_custom_call" | custom-call | tf_op jit(solution)/shard_map/embed/pallas_call | solution.py:75
  3.1 4.6 %collective-permute-start = (bf16[3,128,128]{2,1,0:T(8,128)(2,1)}, bf16[3,128,128]{2,1,0:T(8,128)(2,1)S(1)}, u32[]{:S(2)}, u32[]{:S(2)}) collective-permute-start(bf16[3,128,128]{2,1,0:T(8,128)(2,1)} %get-tuple-element.17), channel_id=1, source_target_pairs={{0,1},{1,2},{2,3},{3,4},{4,5},{5,6},{6,7},{8,9},{9,10},{10,11},{11... | collective-permute-start | bytes 294920 | tf_op jit(solution)/shard_map/ppermute | solution.py:166
  7.7 5.5 %collective-permute-start.1 = (bf16[3,128,128]{2,1,0:T(8,128)(2,1)}, bf16[3,128,128]{2,1,0:T(8,128)(2,1)S(1)}, u32[]{:S(2)}, u32[]{:S(2)}) collective-permute-start(bf16[3,128,128]{2,1,0:T(8,128)(2,1)} %get-tuple-element.18), channel_id=1, source_target_pairs={{1,0},{2,1},{3,2},{4,3},{5,4},{6,5},{7,6},{9,8},{10,9},{11,10},{12... | collective-permute-start | bytes 294920 | tf_op jit(solution)/shard_map/ppermute | solution.py:167
  13.2 0.0 copy-start.4
  13.2 0.9 %copy-done.4 = bf16[3,128,128]{2,1,0:T(8,128)(2,1)S(1)} copy-done((bf16[3,128,128]{2,1,0:T(8,128)(2,1)S(1)}, bf16[3,128,128]{2,1,0:T(8,128)(2,1)}, u32[]{:S(2)}) %copy-start.4) | copy-done | bytes 98328
  14.1 0.0 copy-start.7
  14.1 0.7 %copy-done.7 = bf16[3,3,3,128]{3,2,1,0:T(4,128)(2,1)S(1)} copy-done((bf16[3,3,3,128]{3,2,1,0:T(4,128)(2,1)S(1)}, bf16[3,3,3,128]{3,2,1,0:T(4,128)(2,1)}, u32[]{:S(2)}) %copy-start.7) | copy-done | bytes 6936
  14.8 2.1 %inner.1 = (f32[16,144,128]{2,1,0:T(8,128)S(1)}, f32[16,144,128]{2,1,0:T(8,128)S(1)}, f32[2,128,128]{2,1,0:T(8,128)S(1)}) custom-call(f32[16,144,128]{2,1,0:T(8,128)S(1)} %get-tuple-element.13.hidden_ref, bf16[3,3,3,128]{3,2,1,0:T(4,128)(2,1)S(1)} %copy-done.7, bf16[3,128,128]{2,1,0:T(8,128)(2,1)S(1)} %copy-done.4), custom_call_target="tpu_custom_call" | custom-call | flops 400000000 | bytes 4000000 | tf_op jit(solution)/shard_map/inner/pallas_call | solution.py:171
  16.8 0.1 add_convert_fusion.inside_ref
  16.9 0.0 collective-permute-done.first_ref
  16.9 0.0 collective-permute-done.1.last_ref
  16.9 0.0 copy-start.5
  16.9 0.9 %copy-done.5 = bf16[3,128,128]{2,1,0:T(8,128)(2,1)S(1)} copy-done((bf16[3,128,128]{2,1,0:T(8,128)(2,1)S(1)}, bf16[3,128,128]{2,1,0:T(8,128)(2,1)}, u32[]{:S(2)}) %copy-start.5) | copy-done | bytes 98328
  17.8 0.0 copy-start.8
  17.8 0.7 %copy-done.8 = bf16[3,3,3,128]{3,2,1,0:T(4,128)(2,1)S(1)} copy-done((bf16[3,3,3,128]{3,2,1,0:T(4,128)(2,1)S(1)}, bf16[3,3,3,128]{3,2,1,0:T(4,128)(2,1)}, u32[]{:S(2)}) %copy-start.8) | copy-done | bytes 6936
  18.5 1.7 %outer.1 = bf16[2,16,128]{2,1,0:T(8,128)(2,1)S(1)} custom-call(s32[2]{0:T(128)S(1)} %add_convert_fusion.inside_ref, f32[16,144,128]{2,1,0:T(8,128)S(1)} %get-tuple-element.13.hidden_ref, f32[16,144,128]{2,1,0:T(8,128)S(1)} %get-tuple-element.14.one_ref, f32[16,144,128]{2,1,0:T(8,128)S(1)} %get-tuple-element.15.two_ref, ...), custom_call_target="tpu_custom_call" | custom-call | tf_op jit(solution)/shard_map/outer/pallas_call | solution.py:181
  20.2 0.0 copy-start.2
  20.2 0.0 copy-start.3
  20.3 0.0 copy-start.9
  20.3 0.0 copy-start.10
  20.3 0.0 copy-start.11
  20.3 0.0 copy-start.12
  20.3 0.0 copy-done
  20.3 0.4 convolution_bitcast_fusion
  20.7 28.5 %all_to_all.14 = f32[64,2,128]{2,1,0:T(2,128)S(1)} all-to-all(f32[64,2,128]{2,1,0:T(2,128)S(1)} %broadcast_in_dim.27), channel_id=1, replica_groups=mesh['tm'=64,'tile'=8] {'tm'}, dimensions={0} | all-to-all | bytes 131072 | tf_op jit(solution)/shard_map/all_to_all | solution.py:313
  49.3 0.0 copy-done.2
  49.3 0.0 copy-done.3
  49.3 0.0 copy-done.9
  49.3 0.0 copy-done.10
  49.3 0.0 copy-done.11
  49.3 0.0 copy-done.12
  49.3 2.4 %filter_frames.1 = f32[8,32]{1,0:T(8,128)S(1)} custom-call(s32[1]{0:T(128)} %bitcast.6.frame_ref, f32[128,128]{1,0:T(8,128)S(1)} %bitcast.21, f32[256,256]{1,0:T(8,128)S(1)} %copy-done.2, f32[1,128]{1,0:T(1,128)S(1)} %bitcast.24, f32[1,128]{1,0:T(1,128)S(1)} %bitcast.25, f32[1,128]{1,0:T(1,128)S(1)} %bitcast.26, f32[1,128]{1,0:T(1,128)S(1)} %bitcast.27, ...), custom_call_target="tpu_custom_call" | custom-call | tf_op jit(solution)/shard_map/filter_frames/pallas_call | solution.py:271
  51.7 10.6 %all_to_all.15 = f32[8,1,32]{2,1,0:T(1,128)S(1)} all-to-all(f32[8,1,32]{2,1,0:T(1,128)S(1)} %bitcast.23), channel_id=1, replica_groups=mesh['tm'=64,'tile'=8] {'tile'}, dimensions={0} | all-to-all | bytes 2048 | tf_op jit(solution)/shard_map/all_to_all | solution.py:322
  62.3 0.5 reduce_sum.9
  (1 shorter events, 0.0 us)
Async XLA Ops:
  0.0 20.3 %copy-start = (bf16[2,16,128,256]{3,2,1,0:T(8,128)(2,1)S(1)}, bf16[2,16,128,256]{3,2,1,0:T(8,128)(2,1)}, u32[]{:S(2)}) copy-start(bf16[2,16,128,256]{3,2,1,0:T(8,128)(2,1)} %param.15) | copy-start | bytes 6291460
  0.0 1.1 %copy-start.1 = (bf16[1,1024,128]{2,1,0:T(8,128)(2,1)S(1)}, bf16[1,1024,128]{2,1,0:T(8,128)(2,1)}, u32[]{:S(2)}) copy-start(bf16[1,1024,128]{2,1,0:T(8,128)(2,1)} %frame_ref.1) | copy-start | bytes 786436
  1.1 0.7 %copy-start.6 = (bf16[64,128]{1,0:T(8,128)(2,1)S(1)}, bf16[64,128]{1,0:T(8,128)(2,1)}, u32[]{:S(2)}) copy-start(bf16[64,128]{1,0:T(8,128)(2,1)} %weight_ref.1) | copy-start | bytes 49156
  3.1 13.8 %collective-permute-start = (bf16[3,128,128]{2,1,0:T(8,128)(2,1)}, bf16[3,128,128]{2,1,0:T(8,128)(2,1)S(1)}, u32[]{:S(2)}, u32[]{:S(2)}) collective-permute-start(bf16[3,128,128]{2,1,0:T(8,128)(2,1)} %get-tuple-element.17), channel_id=1, source_target_pairs={{0,1},{1,2},{2,3},{3,4},{4,5},{5,6},{6,7},{8,9},{9,10},{10,11},{11... | collective-permute-start | bytes 294920 | tf_op jit(solution)/shard_map/ppermute | solution.py:166
  7.7 9.2 %collective-permute-start.1 = (bf16[3,128,128]{2,1,0:T(8,128)(2,1)}, bf16[3,128,128]{2,1,0:T(8,128)(2,1)S(1)}, u32[]{:S(2)}, u32[]{:S(2)}) collective-permute-start(bf16[3,128,128]{2,1,0:T(8,128)(2,1)} %get-tuple-element.18), channel_id=1, source_target_pairs={{1,0},{2,1},{3,2},{4,3},{5,4},{6,5},{7,6},{9,8},{10,9},{11,10},{12... | collective-permute-start | bytes 294920 | tf_op jit(solution)/shard_map/ppermute | solution.py:167
  13.2 0.9 %copy-start.4 = (bf16[3,128,128]{2,1,0:T(8,128)(2,1)S(1)}, bf16[3,128,128]{2,1,0:T(8,128)(2,1)}, u32[]{:S(2)}) copy-start(bf16[3,128,128]{2,1,0:T(8,128)(2,1)} %point_ref.3) | copy-start | bytes 294916
  14.1 0.7 %copy-start.7 = (bf16[3,3,3,128]{3,2,1,0:T(4,128)(2,1)S(1)}, bf16[3,3,3,128]{3,2,1,0:T(4,128)(2,1)}, u32[]{:S(2)}) copy-start(bf16[3,3,3,128]{3,2,1,0:T(4,128)(2,1)} %depth_ref.3) | copy-start | bytes 20740
  16.9 0.9 %copy-start.5 = (bf16[3,128,128]{2,1,0:T(8,128)(2,1)S(1)}, bf16[3,128,128]{2,1,0:T(8,128)(2,1)}, u32[]{:S(2)}) copy-start(bf16[3,128,128]{2,1,0:T(8,128)(2,1)} %point_ref.3) | copy-start | bytes 294916
  17.8 0.7 %copy-start.8 = (bf16[3,3,3,128]{3,2,1,0:T(4,128)(2,1)S(1)}, bf16[3,3,3,128]{3,2,1,0:T(4,128)(2,1)}, u32[]{:S(2)}) copy-start(bf16[3,3,3,128]{3,2,1,0:T(4,128)(2,1)} %depth_ref.3) | copy-start | bytes 20740
  20.2 29.0 %copy-start.2 = (f32[256,256]{1,0:T(8,128)S(1)}, f32[256,256]{1,0:T(8,128)}, u32[]{:S(2)}) copy-start(f32[256,256]{1,0:T(8,128)} %input_ref.1) | copy-start | bytes 786436
  20.2 29.0 %copy-start.3 = (f32[256,256]{1,0:T(8,128)S(1)}, f32[256,256]{1,0:T(8,128)}, u32[]{:S(2)}) copy-start(f32[256,256]{1,0:T(8,128)} %readout_ref.1) | copy-start | bytes 786436
  20.3 29.0 %copy-start.9 = (f32[128]{0:T(128)S(1)}, f32[128]{0:T(128)}, u32[]{:S(2)}) copy-start(f32[128]{0:T(128)} %param.17) | copy-start | bytes 1540
  20.3 29.0 %copy-start.10 = (f32[128]{0:T(128)S(1)}, f32[128]{0:T(128)}, u32[]{:S(2)}) copy-start(f32[128]{0:T(128)} %param.18) | copy-start | bytes 1540
  20.3 29.0 %copy-start.11 = (f32[128]{0:T(128)S(1)}, f32[128]{0:T(128)}, u32[]{:S(2)}) copy-start(f32[128]{0:T(128)} %param.19) | copy-start | bytes 1540
  20.3 29.0 %copy-start.12 = (f32[128]{0:T(128)S(1)}, f32[128]{0:T(128)}, u32[]{:S(2)}) copy-start(f32[128]{0:T(128)} %param.20) | copy-start | bytes 1540

commit v3 on v2

--- a/solution.py
+++ b/solution.py
@@ -13,6 +13,8 @@
 PAD = 8
 EDGE = LAYERS
 VMEM = pl.BlockSpec(memory_space=pltpu.VMEM)
+HBM = pl.BlockSpec(memory_space=pltpu.HBM)
+PARTS = 4
 CUBIC = 0.044715
 ROOT = 0.7978845608028654
 
@@ -29,21 +31,40 @@
     ref[at, PAD + rows :, :] = zeros
 
 
-def embed_kernel(frame_ref, weight_ref, hidden_ref, first_ref, last_ref, wide_ref, spread_ref):
-    lanes = frame_ref.shape[2]
-    rows = frame_ref.shape[1] // PATCH
+def embed_kernel(frame_hbm, patch_hbm, depth_hbm, point_hbm, hidden_ref, partner_ref, other_ref, depth_ref,
+                 point_ref, frame_ref, weight_ref, first_ref, last_ref, wide_ref, spread_ref, sems):
+    height, lanes = frame_ref.shape
+    rows = height // PATCH
     channels = weight_ref.shape[1]
     group = 32
     cells = group // PATCH
     columns = lanes // PATCH
-    wide_ref[...] = frame_ref[0].astype(jnp.float32)
+    part = height // PARTS
+    pieces = [
+        pltpu.make_async_copy(
+            frame_hbm.at[0, pl.ds(k * part, part), :], frame_ref.at[pl.ds(k * part, part), :], sems.at[k]
+        )
+        for k in range(PARTS)
+    ]
+    patch = pltpu.make_async_copy(patch_hbm, weight_ref, sems.at[PARTS])
+    depth = pltpu.make_async_copy(depth_hbm, depth_ref, sems.at[PARTS + 1])
+    point = pltpu.make_async_copy(point_hbm, point_ref, sems.at[PARTS + 2])
+    patch.start()
+    for piece in pieces:
+        piece.start()
+    depth.start()
+    point.start()
+    spread_ref[...] = jnp.zeros(spread_ref.shape, spread_ref.dtype)
+    patch.wait()
     weight = weight_ref[...].astype(jnp.float32) * 0.5
-    spread_ref[...] = jnp.zeros(spread_ref.shape, spread_ref.dtype)
     for i in range(PATCH):
         for c in range(cells):
             at = (i * cells + c) * PATCH
             spread_ref[at : at + PATCH, c * channels : (c + 1) * channels] = weight[i * PATCH : (i + 1) * PATCH]
     spread = spread_ref[...].astype(jnp.bfloat16)
+    for k, piece in enumerate(pieces):
+        piece.wait()
+        wide_ref[pl.ds(k * part, part), :] = frame_ref[pl.ds(k * part, part), :].astype(jnp.float32)
     lines = [wide_ref[pl.ds(i, rows, stride=PATCH), :] for i in range(PATCH)]
     lane_group = lax.broadcasted_iota(jnp.int32, (rows, lanes), 1) // group
     per = lanes // group
@@ -66,24 +87,40 @@
                 first_ref[at] = value
             if at >= columns - EDGE:
                 last_ref[at - (columns - EDGE)] = value
-
-
-def embed(frames, patch_weight):
+    odd = lax.rem(lax.axis_index("tile"), 2) == 1
+    partner_ref[...] = jnp.where(odd, first_ref[...], last_ref[...])
+    other_ref[...] = jnp.where(odd, last_ref[...], first_ref[...])
+    depth.wait()
+    point.wait()
+
+
+def embed(frames, patch_weight, depth_weight, point_weight):
     _, height, lanes = frames.shape
     rows, columns, channels = height // PATCH, lanes // PATCH, patch_weight.shape[1]
     edge = jax.ShapeDtypeStruct((EDGE, rows, channels), jnp.bfloat16)
     return pl.pallas_call(
         embed_kernel,
-        out_shape=(jax.ShapeDtypeStruct((columns, rows + 2 * PAD, channels), jnp.float32), edge, edge),
-        in_specs=[VMEM] * 2,
-        out_specs=(VMEM,) * 3,
+        out_shape=(
+            jax.ShapeDtypeStruct((columns, rows + 2 * PAD, channels), jnp.float32),
+            edge,
+            edge,
+            jax.ShapeDtypeStruct(depth_weight.shape, depth_weight.dtype),
+            jax.ShapeDtypeStruct(point_weight.shape, point_weight.dtype),
+        ),
+        in_specs=[HBM] * 4,
+        out_specs=(VMEM,) * 5,
         scratch_shapes=[
+            pltpu.VMEM((height, lanes), frames.dtype),
+            pltpu.VMEM(patch_weight.shape, patch_weight.dtype),
+            pltpu.VMEM(edge.shape, edge.dtype),
+            pltpu.VMEM(edge.shape, edge.dtype),
             pltpu.VMEM((height, lanes), jnp.float32),
             pltpu.VMEM((256, 4 * channels), jnp.float32),
+            pltpu.SemaphoreType.DMA((PARTS + 3,)),
         ],
         compiler_params=pltpu.CompilerParams(vmem_limit_bytes=16 << 20),
         name="embed",
-    )(frames, patch_weight)
+    )(*(pltpu.with_memory_space_constraint(x, pltpu.HBM) for x in (frames, patch_weight, depth_weight, point_weight)))
 
 
 def taps_of(depth_ref, layer):
@@ -118,14 +155,15 @@
                 sum_ref[at // POOL] += value
 
 
-def outer_kernel(inside_ref, hidden_ref, one_ref, two_ref, sum_ref, first_ref, last_ref, depth_ref, point_ref,
+def outer_kernel(hidden_ref, one_ref, two_ref, sum_ref, partner_ref, other_ref, depth_ref, point_ref,
                  pooled_ref, border_ref):
     columns = hidden_ref.shape[0]
     taps = [taps_of(depth_ref, layer) for layer in range(LAYERS)]
     weights = [(point_ref[layer].astype(jnp.float32) * 0.5).astype(jnp.bfloat16) for layer in range(LAYERS)]
-    inside = (inside_ref[0].astype(jnp.float32), inside_ref[1].astype(jnp.float32))
-    for side in range(2):
-        halo = (first_ref, last_ref)[side]
+    here, size = lax.axis_index("tile"), lax.axis_size("tile")
+    odd = lax.rem(here, 2)
+    inside = ((here > 0).astype(jnp.float32), (here < size - 1).astype(jnp.float32))
+    for halo, side in ((partner_ref, 1 - odd), (other_ref, odd)):
         for k in range(EDGE):
             put_column(border_ref.at[side, 0], k, halo[k].astype(jnp.float32))
 
@@ -160,11 +198,13 @@
 
 
 def encode(frames, patch_weight, depth_weight, point_weight):
-    size, here = lax.axis_size("tile"), lax.axis_index("tile")
-    hidden, first, last = embed(frames, patch_weight)
-    up = [(i, i + 1) for i in range(size - 1)]
-    before = lax.ppermute(last, "tile", up)
-    after = lax.ppermute(first, "tile", [(j, i) for i, j in up])
+    size = lax.axis_size("tile")
+    hidden, partner, other, depth_weight, point_weight = embed(
+        frames, patch_weight, depth_weight, point_weight
+    )
+    partner = lax.ppermute(partner, "tile", [(i, i ^ 1) for i in range(size)])
+    pairs = [(i, i + 1) for i in range(1, size - 1, 2)]
+    other = lax.ppermute(other, "tile", pairs + [(j, i) for i, j in pairs])
     columns, padded, channels = hidden.shape
     rows = padded - 2 * PAD
     level = jax.ShapeDtypeStruct(hidden.shape, jnp.float32)
@@ -177,25 +217,33 @@
         cost_estimate=pl.CostEstimate(flops=400_000_000, bytes_accessed=4_000_000, transcendentals=0),
         name="inner",
     )(hidden, depth_weight, point_weight)
-    inside = jnp.stack([here > 0, here < size - 1]).astype(jnp.int32)
     return pl.pallas_call(
         outer_kernel,
         out_shape=jax.ShapeDtypeStruct((2, rows // POOL, channels), jnp.bfloat16),
-        in_specs=[pl.BlockSpec(memory_space=pltpu.SMEM)] + [VMEM] * 8,
+        in_specs=[VMEM] * 8,
         out_specs=VMEM,
         scratch_shapes=[pltpu.VMEM((2, LAYERS, EDGE, padded, channels), jnp.float32)],
         compiler_params=pltpu.CompilerParams(vmem_limit_bytes=20 << 20),
         name="outer",
-    )(inside, hidden, one, two, total, before, after, depth_weight, point_weight)
-
-
-HIGHEST = lax.Precision.HIGHEST
+    )(hidden, one, two, total, partner, other, depth_weight, point_weight)
+
+
+def in_two(x):
+    high = x.astype(jnp.bfloat16)
+    return high, (x - high.astype(jnp.float32)).astype(jnp.bfloat16)
 
 
 def dot_t(a, b):
-    return lax.dot_general(
-        a, b, (((1,), (1,)), ((), ())), precision=HIGHEST, preferred_element_type=jnp.float32
-    )
+    def dot(u, v):
+        return lax.dot_general(u, v, (((1,), (1,)), ((), ())), preferred_element_type=jnp.float32)
+
+    a_high, a_low = in_two(a)
+    b_high, b_low = in_two(b)
+    return dot(a_low, b_high) + dot(a_high, b_low) + dot(a_high, b_high)
+
+
+def lanes_at(x, index):
+    return jnp.take_along_axis(x, index, axis=1, mode="promise_in_bounds")
 
 
 def scan_rows(real, imag, mult_real, mult_imag, backward):
@@ -219,26 +267,22 @@
     return real, imag
 
 
-def filter_kernel(frame_ref, seen_ref, input_ref, decay_ref, angle_ref, back_decay_ref, back_angle_ref,
-                  readout_ref, out_ref):
+def filter_kernel(seen_ref, input_ref, decay_ref, angle_ref, back_decay_ref, back_angle_ref, readout_ref, out_ref):
     modes = decay_ref.shape[1]
     parts = input_ref.shape[1] // seen_ref.shape[1]
     frames = seen_ref.shape[0] // parts
-    lanes = seen_ref.shape[1]
     decay, angle = decay_ref[...], angle_ref[...]
     back_decay, back_angle = back_decay_ref[...], back_angle_ref[...]
     gain = jnp.sqrt(1.0 - decay * decay)
     back_gain = jnp.sqrt(1.0 - back_decay * back_decay)
-    mode = lax.broadcasted_iota(jnp.int32, (modes, 2 * modes), 0)
-    place = lax.broadcasted_iota(jnp.int32, (modes, 2 * modes), 1)
-    real_place = (place == 2 * mode).astype(jnp.float32)
-    imag_place = (place == 2 * mode + 1).astype(jnp.float32)
-    drive = sum(
-        dot_t(seen_ref[pl.ds(k, frames, stride=parts), :], input_ref[:, k * lanes : (k + 1) * lanes])
-        for k in range(parts)
-    )
-    real = dot_t(drive, real_place) * gain
-    imag = dot_t(drive, imag_place) * gain
+    seen = jnp.concatenate([seen_ref[pl.ds(k, frames, stride=parts), :] for k in range(parts)], axis=1)
+    drive = dot_t(seen, input_ref[...])
+    lower, upper = drive[:, :modes], drive[:, modes:]
+    lane = lax.broadcasted_iota(jnp.int32, (frames, modes), 1)
+    even = lax.rem(2 * lane, modes)
+    in_lower = lane < modes // 2
+    real = jnp.where(in_lower, lanes_at(lower, even), lanes_at(upper, even)) * gain
+    imag = jnp.where(in_lower, lanes_at(lower, even + 1), lanes_at(upper, even + 1)) * gain
     real, imag = scan_rows(real, imag, decay * jnp.cos(angle), decay * jnp.sin(angle), False)
     real, imag = scan_rows(
         real * back_gain,
@@ -247,17 +291,18 @@
         back_decay * jnp.sin(back_angle),
         True,
     )
-    mine = lax.broadcasted_iota(jnp.int32, real.shape, 0) == frame_ref[0]
-    real = jnp.sum(jnp.where(mine, real, 0.0), axis=0, keepdims=True)
-    imag = jnp.sum(jnp.where(mine, imag, 0.0), axis=0, keepdims=True)
+    mine = lax.broadcasted_iota(jnp.int32, real.shape, 0) == lax.axis_index("tm")
     shares = out_ref.shape[0]
     width = out_ref.shape[1]
-    real = jnp.broadcast_to(real, (shares, modes))
-    imag = jnp.broadcast_to(imag, (shares, modes))
-    laid = jnp.dot(
-        real, real_place, precision=HIGHEST
-    ) + jnp.dot(imag, imag_place, precision=HIGHEST)
-    latent = dot_t(laid, readout_ref[...])
+    real = jnp.broadcast_to(jnp.sum(jnp.where(mine, real, 0.0), axis=0, keepdims=True), (shares, modes))
+    imag = jnp.broadcast_to(jnp.sum(jnp.where(mine, imag, 0.0), axis=0, keepdims=True), (shares, modes))
+    lane = lax.broadcasted_iota(jnp.int32, (shares, modes), 1)
+    mode = lane // 2
+    is_real = lane == 2 * mode
+    laid = [
+        jnp.where(is_real, lanes_at(real, mode + at), lanes_at(imag, mode + at)) for at in (0, modes // 2)
+    ]
+    latent = dot_t(jnp.concatenate(laid, axis=1), readout_ref[...])
     share = lax.broadcasted_iota(jnp.int32, (shares, width), 0)
     out = latent[:, :width]
     for k in range(1, shares):
@@ -265,18 +310,16 @@
     out_ref[...] = out
 
 
-def filter_frames(frame, seen, input_map, mode_decay, mode_angle, smooth_decay, smooth_angle, readout, shares):
-    vmem = pl.BlockSpec(memory_space=pltpu.VMEM)
+def filter_frames(seen, input_map, mode_decay, mode_angle, smooth_decay, smooth_angle, readout, shares):
     width = readout.shape[0] // shares
     return pl.pallas_call(
         filter_kernel,
         out_shape=jax.ShapeDtypeStruct((shares, width), jnp.float32),
-        in_specs=[pl.BlockSpec(memory_space=pltpu.SMEM)] + [vmem] * 7,
-        out_specs=vmem,
+        in_specs=[VMEM] * 7,
+        out_specs=VMEM,
         compiler_params=pltpu.CompilerParams(vmem_limit_bytes=8 << 20),
         name="filter_frames",
     )(
-        frame,
         seen,
         input_map,
         mode_decay[None],
@@ -307,9 +350,7 @@
         preferred_element_type=jnp.float32,
     )
     frames = lax.axis_size("tm")
-    partial_value, frame = lax.optimization_barrier(
-        (partial_value, lax.axis_index("tm").astype(jnp.int32)[None])
-    )
+    partial_value = lax.optimization_barrier(partial_value)
     seen = lax.all_to_all(
         jnp.broadcast_to(partial_value.reshape(1, -1, 128), (frames, partial_value.shape[1] // 128, 128)),
         "tm",
@@ -317,7 +358,7 @@
         0,
     ).reshape(-1, 128)
     shares = filter_frames(
-        frame, seen, input_map, mode_decay, mode_angle, smooth_decay, smooth_angle, readout, tile_count
+        seen, input_map, mode_decay, mode_angle, smooth_decay, smooth_angle, readout, tile_count
     )
     terms = lax.all_to_all(shares, "tile", 0, 0)
     return jnp.sum(terms, axis=0, keepdims=True)

time: 63.3 us -> 57.6 us (0.910)
  local copies, waits for them, and re-layouts: 5.06 us -> 0.07 us
  blocking collectives: 39.1 us -> 37.1 us
  waiting for transfers between devices: 0.01 us -> 1.88 us
  Pallas kernels: 7.44 us -> 6.56 us
  starting transfers between devices: 10 us -> 10.7 us
    unnamed x26 -> x14, local copies, waits for them, and re-layouts: 5.04 us -> 0.04 us
    all_to_all x1, blocking collectives: 28.5 us -> 26.3 us  [shards(): lax.all_to_all(jnp.broadcast_to(partial_value.reshape(1, -1, 128), (frame...]
    ppermute x2, waiting for transfers between devices: 0.01 us -> 1.88 us  [the longest x1 1.88 us: encode(): other = lax.ppermute(other, 'tile', pairs + [(j, i) for i, j in pairs])]
    pallas_call x1, Pallas kernels: 2.36 us -> 1.43 us  [filter_frames(): pl.pallas_call(filter_kernel, out_shape=jax.ShapeDtypeStruct((shares, wid...]
    ppermute x2, starting transfers between devices: 10 us -> 10.7 us  [the longest x1 8.75 us: encode(): partner = lax.ppermute(partner, 'tile', [(i, i ^ 1) for i in range(size)])]
  transfers between devices with their start and end apart: 2 -> 2, of which waited for: 0 -> 1; matrix products, arithmetic and copies ran while one was open for 0% -> 0% of each run, Pallas kernels for 3% -> 4%
where the time goes in v3:
time: 57.6 us; the launch traced here: 57.3 us
  blocking collectives  37.1 us (64%)
  starting transfers between devices  10.7 us (19%)
  Pallas kernels  6.56 us (11%)
  waiting for transfers between devices  1.88 us (3%)
    all_to_all x1, blocking collectives, shards(): lax.all_to_all(jnp.broadcast_to(partial_value.reshape(1, -1, 128), (frame...  26.3 us
    all_to_all x1, blocking collectives, shards(): terms = lax.all_to_all(shares, 'tile', 0, 0)  10.9 us
    ppermute x1, starting transfers between devices, encode(): partner = lax.ppermute(partner, 'tile', [(i, i ^ 1) for i in range(size)])  8.75 us
    pallas_call x1, Pallas kernels, encode(): pl.pallas_call(inner_kernel, out_shape=(level, level, jax.ShapeDtypeStruc...  2.12 us
    ppermute x1, starting transfers between devices, encode(): other = lax.ppermute(other, 'tile', pairs + [(j, i) for i, j in pairs])  1.92 us
    ppermute x1, waiting for transfers between devices, encode(): other = lax.ppermute(other, 'tile', pairs + [(j, i) for i, j in pairs])  1.88 us
    pallas_call x1, Pallas kernels, embed(): pl.pallas_call(embed_kernel, out_shape=(jax.ShapeDtypeStruct((columns, ro...  1.83 us
    pallas_call x1, Pallas kernels, filter_frames(): pl.pallas_call(filter_kernel, out_shape=jax.ShapeDtypeStruct((shares, wid...  1.43 us
  transfers between devices with their start and end apart: 2, of which 1 were waited for; matrix products, arithmetic and copies ran while one was open for 0% of the time, Pallas kernels for 4%

profile of v3, /device:TPU:1, one launch (start us, length us, event | category | flops | bytes accessed | tf_op | source)
XLA Modules:
  0.0 57.3 jit_solution(14965759797073806179)
XLA Ops:
  0.0 0.0 copy-start
  0.0 1.8 %embed.1 = (f32[16,144,128]{2,1,0:T(8,128)S(1)}, bf16[3,128,128]{2,1,0:T(8,128)(2,1)S(1)}, bf16[3,128,128]{2,1,0:T(8,128)(2,1)S(1)}, bf16[3,3,3,128]{3,2,1,0:T(4,128)(2,1)S(1)}, bf16[3,128,128]{2,1,0:T(8,128)(2,1)S(1)}) custom-call(bf16[1,1024,128]{2,1,0:T(8,128)(2,1)} %frame_hbm.1, bf16[64,128]{1,0:T(8,128)(2,1)} %patch_hbm.1, ...), custom_call_target="tpu_custom_call" | custom-call | tf_op jit(solution)/shard_map/embed/pallas_call | solution.py:101
  1.8 8.7 %collective-permute-start = (bf16[3,128,128]{2,1,0:T(8,128)(2,1)S(1)}, bf16[3,128,128]{2,1,0:T(8,128)(2,1)S(1)}, u32[]{:S(2)}, u32[]{:S(2)}) collective-permute-start(bf16[3,128,128]{2,1,0:T(8,128)(2,1)S(1)} %get-tuple-element.19), channel_id=1, source_target_pairs={{0,1},{1,0},{2,3},{3,2},{4,5},{5,4},{6,7},{7,6},{8,9},{9,8},{10,11... | collective-permute-start | bytes 294920 | tf_op jit(solution)/shard_map/ppermute | solution.py:205
  10.6 1.9 %collective-permute-start.1 = (bf16[3,128,128]{2,1,0:T(8,128)(2,1)S(1)}, bf16[3,128,128]{2,1,0:T(8,128)(2,1)S(1)}, u32[]{:S(2)}, u32[]{:S(2)}) collective-permute-start(bf16[3,128,128]{2,1,0:T(8,128)(2,1)S(1)} %get-tuple-element.20), channel_id=1, source_target_pairs={{1,2},{3,4},{5,6},{2,1},{4,3},{6,5},{9,10},{11,12},{13,14},{10,9},... | collective-permute-start | bytes 294920 | tf_op jit(solution)/shard_map/ppermute | solution.py:207
  12.5 2.1 %inner.1 = (f32[16,144,128]{2,1,0:T(8,128)S(1)}, f32[16,144,128]{2,1,0:T(8,128)S(1)}, f32[2,128,128]{2,1,0:T(8,128)S(1)}) custom-call(f32[16,144,128]{2,1,0:T(8,128)S(1)} %get-tuple-element.13.hidden_ref, bf16[3,3,3,128]{3,2,1,0:T(4,128)(2,1)S(1)} %get-tuple-element.14.depth_ref, bf16[3,128,128]{2,1,0:T(8,128)(2,1)S(1)} %get-tuple-element.15.point_ref), custom_call_target="tpu_custom_call" | custom-call | flops 400000000 | bytes 4000000 | tf_op jit(solution)/shard_map/inner/pallas_call | solution.py:211
  14.6 0.0 collective-permute-done.partner_ref
  14.7 1.9 %collective-permute-done.1.other_ref = bf16[3,128,128]{2,1,0:T(8,128)(2,1)S(1)} collective-permute-done((bf16[3,128,128]{2,1,0:T(8,128)(2,1)S(1)}, bf16[3,128,128]{2,1,0:T(8,128)(2,1)S(1)}, u32[]{:S(2)}, u32[]{:S(2)}) %collective-permute-start.1) | collective-permute-done | bytes 98336 | tf_op jit(solution)/shard_map/ppermute | solution.py:207
  16.5 1.2 %outer.1 = bf16[2,16,128]{2,1,0:T(8,128)(2,1)S(1)} custom-call(f32[16,144,128]{2,1,0:T(8,128)S(1)} %get-tuple-element.13.hidden_ref, f32[16,144,128]{2,1,0:T(8,128)S(1)} %get-tuple-element.16.one_ref, f32[16,144,128]{2,1,0:T(8,128)S(1)} %get-tuple-element.17.two_ref, f32[2,128,128]{2,1,0:T(8,128)S(1)} %get-tuple-element.18.sum_ref, ...), custom_call_target="tpu_custom_call" | custom-call | tf_op jit(solution)/shard_map/outer/pallas_call | solution.py:220
  17.7 0.0 copy-start.1
  17.7 0.0 copy-start.2
  17.7 0.0 copy-start.3
  17.8 0.0 copy-start.4
  17.8 0.0 copy-start.5
  17.8 0.0 copy-start.6
  17.8 0.0 copy-done
  17.8 0.4 convolution_bitcast_fusion
  18.2 26.3 %all_to_all.14 = f32[64,2,128]{2,1,0:T(2,128)S(1)} all-to-all(f32[64,2,128]{2,1,0:T(2,128)S(1)} %broadcast_in_dim.23), channel_id=1, replica_groups=mesh['tm'=64,'tile'=8] {'tm'}, dimensions={0} | all-to-all | bytes 131072 | tf_op jit(solution)/shard_map/all_to_all | solution.py:354
  44.5 0.0 copy-done.1
  44.5 0.0 copy-done.2
  44.5 0.0 copy-done.3
  44.5 0.0 copy-done.4
  44.5 0.0 copy-done.5
  44.5 0.0 copy-done.6
  44.5 1.4 %filter_frames.1 = f32[8,32]{1,0:T(8,128)S(1)} custom-call(f32[128,128]{1,0:T(8,128)S(1)} %bitcast.18, f32[256,256]{1,0:T(8,128)S(1)} %copy-done.1, f32[1,128]{1,0:T(1,128)S(1)} %bitcast.21, f32[1,128]{1,0:T(1,128)S(1)} %bitcast.22, f32[1,128]{1,0:T(1,128)S(1)} %bitcast.23, f32[1,128]{1,0:T(1,128)S(1)} %bitcast.24, f32[256,256]{1,0:T(8,128)S(1)} %copy-done.2), custom_call_target="tpu_custom_call" | custom-call | tf_op jit(solution)/shard_map/filter_frames/pallas_call | solution.py:315
  45.9 10.9 %all_to_all.15 = f32[8,1,32]{2,1,0:T(1,128)S(1)} all-to-all(f32[8,1,32]{2,1,0:T(1,128)S(1)} %bitcast.20), channel_id=1, replica_groups=mesh['tm'=64,'tile'=8] {'tile'}, dimensions={0} | all-to-all | bytes 2048 | tf_op jit(solution)/shard_map/all_to_all | solution.py:363
  56.8 0.5 reduce_sum.9
  (1 shorter events, 0.0 us)
Async XLA Ops:
  0.0 17.8 %copy-start = (bf16[2,16,128,256]{3,2,1,0:T(8,128)(2,1)S(1)}, bf16[2,16,128,256]{3,2,1,0:T(8,128)(2,1)}, u32[]{:S(2)}) copy-start(bf16[2,16,128,256]{3,2,1,0:T(8,128)(2,1)} %param.15) | copy-start | bytes 6291460
  1.8 12.8 %collective-permute-start = (bf16[3,128,128]{2,1,0:T(8,128)(2,1)S(1)}, bf16[3,128,128]{2,1,0:T(8,128)(2,1)S(1)}, u32[]{:S(2)}, u32[]{:S(2)}) collective-permute-start(bf16[3,128,128]{2,1,0:T(8,128)(2,1)S(1)} %get-tuple-element.19), channel_id=1, source_target_pairs={{0,1},{1,0},{2,3},{3,2},{4,5},{5,4},{6,7},{7,6},{8,9},{9,8},{10,11... | collective-permute-start | bytes 294920 | tf_op jit(solution)/shard_map/ppermute | solution.py:205
  10.6 5.9 %collective-permute-start.1 = (bf16[3,128,128]{2,1,0:T(8,128)(2,1)S(1)}, bf16[3,128,128]{2,1,0:T(8,128)(2,1)S(1)}, u32[]{:S(2)}, u32[]{:S(2)}) collective-permute-start(bf16[3,128,128]{2,1,0:T(8,128)(2,1)S(1)} %get-tuple-element.20), channel_id=1, source_target_pairs={{1,2},{3,4},{5,6},{2,1},{4,3},{6,5},{9,10},{11,12},{13,14},{10,9},... | collective-permute-start | bytes 294920 | tf_op jit(solution)/shard_map/ppermute | solution.py:207
  17.7 26.8 %copy-start.1 = (f32[256,256]{1,0:T(8,128)S(1)}, f32[256,256]{1,0:T(8,128)}, u32[]{:S(2)}) copy-start(f32[256,256]{1,0:T(8,128)} %input_ref.1) | copy-start | bytes 786436
  17.7 26.7 %copy-start.2 = (f32[256,256]{1,0:T(8,128)S(1)}, f32[256,256]{1,0:T(8,128)}, u32[]{:S(2)}) copy-start(f32[256,256]{1,0:T(8,128)} %readout_ref.1) | copy-start | bytes 786436
  17.7 26.7 %copy-start.3 = (f32[128]{0:T(128)S(1)}, f32[128]{0:T(128)}, u32[]{:S(2)}) copy-start(f32[128]{0:T(128)} %param.17) | copy-start | bytes 1540
  17.8 26.7 %copy-start.4 = (f32[128]{0:T(128)S(1)}, f32[128]{0:T(128)}, u32[]{:S(2)}) copy-start(f32[128]{0:T(128)} %param.18) | copy-start | bytes 1540
  17.8 26.7 %copy-start.5 = (f32[128]{0:T(128)S(1)}, f32[128]{0:T(128)}, u32[]{:S(2)}) copy-start(f32[128]{0:T(128)} %param.19) | copy-start | bytes 1540
  17.8 26.7 %copy-start.6 = (f32[128]{0:T(128)S(1)}, f32[128]{0:T(128)}, u32[]{:S(2)}) copy-start(f32[128]{0:T(128)} %param.20) | copy-start | bytes 1540

commit v4 on v3

--- a/solution.py
+++ b/solution.py
@@ -3,11 +3,13 @@
 from jax import lax
 from jax.experimental import pallas as pl
 from jax.experimental.pallas import tpu as pltpu
+from jax.sharding import Mesh
 from jax.sharding import PartitionSpec as P
 
 PATCH = 8
 POOL = 8
 LAYERS = 3
+BLOCKS = 4
 
 
 PAD = 8
@@ -202,10 +204,10 @@
     hidden, partner, other, depth_weight, point_weight = embed(
         frames, patch_weight, depth_weight, point_weight
     )
-    partner = lax.ppermute(partner, "tile", [(i, i ^ 1) for i in range(size)])
     pairs = [(i, i + 1) for i in range(1, size - 1, 2)]
     other = lax.ppermute(other, "tile", pairs + [(j, i) for i, j in pairs])
-    columns, padded, channels = hidden.shape
+    partner = lax.ppermute(partner, "tile", [(i, i ^ 1) for i in range(size)])
+    _, padded, channels = hidden.shape
     rows = padded - 2 * PAD
     level = jax.ShapeDtypeStruct(hidden.shape, jnp.float32)
     one, two, total = pl.pallas_call(
@@ -283,6 +285,11 @@
     in_lower = lane < modes // 2
     real = jnp.where(in_lower, lanes_at(lower, even), lanes_at(upper, even)) * gain
     imag = jnp.where(in_lower, lanes_at(lower, even + 1), lanes_at(upper, even + 1)) * gain
+    blocks = lax.axis_size("x")
+    row = lax.broadcasted_iota(jnp.int32, (blocks * frames, modes), 0)
+    placed = row // frames == lax.axis_index("x")
+    real = jnp.where(placed, jnp.concatenate([real] * blocks, axis=0), 0.0)
+    imag = jnp.where(placed, jnp.concatenate([imag] * blocks, axis=0), 0.0)
     real, imag = scan_rows(real, imag, decay * jnp.cos(angle), decay * jnp.sin(angle), False)
     real, imag = scan_rows(
         real * back_gain,
@@ -291,12 +298,15 @@
         back_decay * jnp.sin(back_angle),
         True,
     )
-    mine = lax.broadcasted_iota(jnp.int32, real.shape, 0) == lax.axis_index("tm")
-    shares = out_ref.shape[0]
-    width = out_ref.shape[1]
-    real = jnp.broadcast_to(jnp.sum(jnp.where(mine, real, 0.0), axis=0, keepdims=True), (shares, modes))
-    imag = jnp.broadcast_to(jnp.sum(jnp.where(mine, imag, 0.0), axis=0, keepdims=True), (shares, modes))
-    lane = lax.broadcasted_iota(jnp.int32, (shares, modes), 1)
+    length = lax.axis_size("z")
+    mine = lax.rem(row, length) == lax.axis_index("z")
+    shares, width = out_ref.shape[0] // blocks, out_ref.shape[1]
+    real = jnp.sum(jnp.where(mine, real, 0.0).reshape(blocks, length, modes), axis=1)
+    imag = jnp.sum(jnp.where(mine, imag, 0.0).reshape(blocks, length, modes), axis=1)
+    if blocks < 8:
+        real = jnp.concatenate([real] * (8 // blocks), axis=0)
+        imag = jnp.concatenate([imag] * (8 // blocks), axis=0)
+    lane = lax.broadcasted_iota(jnp.int32, real.shape, 1)
     mode = lane // 2
     is_real = lane == 2 * mode
     laid = [
@@ -304,17 +314,18 @@
     ]
     latent = dot_t(jnp.concatenate(laid, axis=1), readout_ref[...])
     share = lax.broadcasted_iota(jnp.int32, (shares, width), 0)
-    out = latent[:, :width]
-    for k in range(1, shares):
-        out = jnp.where(share == k, latent[:, k * width : (k + 1) * width], out)
-    out_ref[...] = out
+    for block in range(blocks):
+        out = jnp.broadcast_to(latent[block : block + 1, :width], (shares, width))
+        for k in range(1, shares):
+            out = jnp.where(share == k, latent[block : block + 1, k * width : (k + 1) * width], out)
+        out_ref[block * shares : (block + 1) * shares, :] = out
 
 
 def filter_frames(seen, input_map, mode_decay, mode_angle, smooth_decay, smooth_angle, readout, shares):
     width = readout.shape[0] // shares
     return pl.pallas_call(
         filter_kernel,
-        out_shape=jax.ShapeDtypeStruct((shares, width), jnp.float32),
+        out_shape=jax.ShapeDtypeStruct((lax.axis_size("x") * shares, width), jnp.float32),
         in_specs=[VMEM] * 7,
         out_specs=VMEM,
         compiler_params=pltpu.CompilerParams(vmem_limit_bytes=8 << 20),
@@ -349,24 +360,25 @@
         observe_weight.reshape(-1, observe_weight.shape[-1]),
         preferred_element_type=jnp.float32,
     )
-    frames = lax.axis_size("tm")
+    length = lax.axis_size("z")
     partial_value = lax.optimization_barrier(partial_value)
     seen = lax.all_to_all(
-        jnp.broadcast_to(partial_value.reshape(1, -1, 128), (frames, partial_value.shape[1] // 128, 128)),
-        "tm",
+        jnp.broadcast_to(partial_value.reshape(1, -1, 128), (length, partial_value.shape[1] // 128, 128)),
+        "z",
         0,
         0,
     ).reshape(-1, 128)
     shares = filter_frames(
         seen, input_map, mode_decay, mode_angle, smooth_decay, smooth_angle, readout, tile_count
     )
-    terms = lax.all_to_all(shares, "tile", 0, 0)
+    terms = lax.all_to_all(shares, ("x", "tile"), 0, 0)
     return jnp.sum(terms, axis=0, keepdims=True)
 
 
 def solution(mesh):
+    grid = Mesh(mesh.devices.reshape(BLOCKS, -1, mesh.shape["tile"]), ("x", "z", "tile"))
     placed = (
-        P("tm", None, "tile"),
+        P(("x", "z"), None, "tile"),
         P(),
         P(),
         P(),
@@ -379,5 +391,5 @@
         P(),
     )
     return jax.shard_map(
-        shards, mesh=mesh, in_specs=placed, out_specs=P("tm", "tile"), check_vma=False
-    )
+        shards, mesh=grid, in_specs=placed, out_specs=P(("x", "z"), "tile"), check_vma=False
+    )

time: 57.6 us -> 56.4 us (0.979)
  blocking collectives: 37.1 us -> 36 us
    all_to_all x2, blocking collectives: 37.1 us -> 36 us  [the longest x1 20.8 us: shards(): lax.all_to_all(jnp.broadcast_to(partial_value.reshape(1, -1, 128), (lengt...]
where the time goes in v4:
time: 56.4 us; the launch traced here: 56.2 us
  blocking collectives  36 us (64%)
  starting transfers between devices  10.7 us (19%)
  Pallas kernels  6.52 us (12%)
  waiting for transfers between devices  1.88 us (3%)
    all_to_all x1, blocking collectives, shards(): lax.all_to_all(jnp.broadcast_to(partial_value.reshape(1, -1, 128), (lengt...  20.8 us
    all_to_all x1, blocking collectives, shards(): terms = lax.all_to_all(shares, ('x', 'tile'), 0, 0)  15.3 us
    ppermute x1, starting transfers between devices, encode(): partner = lax.ppermute(partner, 'tile', [(i, i ^ 1) for i in range(size)])  8.75 us
    pallas_call x1, Pallas kernels, encode(): pl.pallas_call(inner_kernel, out_shape=(level, level, jax.ShapeDtypeStruc...  2.12 us
    ppermute x1, starting transfers between devices, encode(): other = lax.ppermute(other, 'tile', pairs + [(j, i) for i, j in pairs])  1.92 us
    ppermute x1, waiting for transfers between devices, encode(): other = lax.ppermute(other, 'tile', pairs + [(j, i) for i, j in pairs])  1.88 us
    pallas_call x1, Pallas kernels, embed(): pl.pallas_call(embed_kernel, out_shape=(jax.ShapeDtypeStruct((columns, ro...  1.83 us
    pallas_call x1, Pallas kernels, filter_frames(): pl.pallas_call(filter_kernel, out_shape=jax.ShapeDtypeStruct((lax.axis_si...  1.39 us
  transfers between devices with their start and end apart: 2, of which 1 were waited for; matrix products, arithmetic and copies ran while one was open for 0% of the time, Pallas kernels for 4%

profile of v4, /device:TPU:1, one launch (start us, length us, event | category | flops | bytes accessed | tf_op | source)
XLA Modules:
  0.0 56.2 jit_solution(351775962515851836)
XLA Ops:
  0.0 0.0 copy-start
  0.0 1.8 %embed.1 = (f32[16,144,128]{2,1,0:T(8,128)S(1)}, bf16[3,128,128]{2,1,0:T(8,128)(2,1)S(1)}, bf16[3,128,128]{2,1,0:T(8,128)(2,1)S(1)}, bf16[3,3,3,128]{3,2,1,0:T(4,128)(2,1)S(1)}, bf16[3,128,128]{2,1,0:T(8,128)(2,1)S(1)}) custom-call(bf16[1,1024,128]{2,1,0:T(8,128)(2,1)} %frame_hbm.1, bf16[64,128]{1,0:T(8,128)(2,1)} %patch_hbm.1, ...), custom_call_target="tpu_custom_call" | custom-call | tf_op jit(solution)/shard_map/embed/pallas_call | solution.py:103
  1.8 8.7 %collective-permute-start = (bf16[3,128,128]{2,1,0:T(8,128)(2,1)S(1)}, bf16[3,128,128]{2,1,0:T(8,128)(2,1)S(1)}, u32[]{:S(2)}, u32[]{:S(2)}) collective-permute-start(bf16[3,128,128]{2,1,0:T(8,128)(2,1)S(1)} %get-tuple-element.19), channel_id=1, source_target_pairs={{0,1},{1,0},{2,3},{3,2},{4,5},{5,4},{6,7},{7,6},{8,9},{9,8},{10,11... | collective-permute-start | bytes 294920 | tf_op jit(solution)/shard_map/ppermute | solution.py:209
  10.6 1.9 %collective-permute-start.1 = (bf16[3,128,128]{2,1,0:T(8,128)(2,1)S(1)}, bf16[3,128,128]{2,1,0:T(8,128)(2,1)S(1)}, u32[]{:S(2)}, u32[]{:S(2)}) collective-permute-start(bf16[3,128,128]{2,1,0:T(8,128)(2,1)S(1)} %get-tuple-element.20), channel_id=1, source_target_pairs={{1,2},{3,4},{5,6},{2,1},{4,3},{6,5},{9,10},{11,12},{13,14},{10,9},... | collective-permute-start | bytes 294920 | tf_op jit(solution)/shard_map/ppermute | solution.py:208
  12.5 2.1 %inner.1 = (f32[16,144,128]{2,1,0:T(8,128)S(1)}, f32[16,144,128]{2,1,0:T(8,128)S(1)}, f32[2,128,128]{2,1,0:T(8,128)S(1)}) custom-call(f32[16,144,128]{2,1,0:T(8,128)S(1)} %get-tuple-element.13.hidden_ref, bf16[3,3,3,128]{3,2,1,0:T(4,128)(2,1)S(1)} %get-tuple-element.14.depth_ref, bf16[3,128,128]{2,1,0:T(8,128)(2,1)S(1)} %get-tuple-element.15.point_ref), custom_call_target="tpu_custom_call" | custom-call | flops 400000000 | bytes 4000000 | tf_op jit(solution)/shard_map/inner/pallas_call | solution.py:213
  14.6 0.0 collective-permute-done.partner_ref
  14.7 1.9 %collective-permute-done.1.other_ref = bf16[3,128,128]{2,1,0:T(8,128)(2,1)S(1)} collective-permute-done((bf16[3,128,128]{2,1,0:T(8,128)(2,1)S(1)}, bf16[3,128,128]{2,1,0:T(8,128)(2,1)S(1)}, u32[]{:S(2)}, u32[]{:S(2)}) %collective-permute-start.1) | collective-permute-done | bytes 98336 | tf_op jit(solution)/shard_map/ppermute | solution.py:208
  16.5 0.0 copy-start.1
  16.5 0.0 copy-start.2
  16.5 0.0 copy-start.3
  16.5 0.0 copy-start.4
  16.5 0.0 copy-start.5
  16.6 0.0 copy-start.6
  16.6 1.2 %outer.1 = bf16[2,16,128]{2,1,0:T(8,128)(2,1)S(1)} custom-call(f32[16,144,128]{2,1,0:T(8,128)S(1)} %get-tuple-element.13.hidden_ref, f32[16,144,128]{2,1,0:T(8,128)S(1)} %get-tuple-element.16.one_ref, f32[16,144,128]{2,1,0:T(8,128)S(1)} %get-tuple-element.17.two_ref, f32[2,128,128]{2,1,0:T(8,128)S(1)} %get-tuple-element.18.sum_ref, ...), custom_call_target="tpu_custom_call" | custom-call | tf_op jit(solution)/shard_map/outer/pallas_call | solution.py:222
  17.8 0.0 copy-done
  17.8 0.4 convolution_bitcast_fusion
  18.2 20.8 %all_to_all.14 = f32[16,2,128]{2,1,0:T(2,128)S(1)} all-to-all(f32[16,2,128]{2,1,0:T(2,128)S(1)} %broadcast_in_dim.23), channel_id=1, replica_groups=mesh['x'=4,'z'=16,'tile'=8] {'z'}, dimensions={0} | all-to-all | bytes 32768 | tf_op jit(solution)/shard_map/all_to_all | solution.py:365
  38.9 0.0 copy-done.1
  38.9 0.0 copy-done.2
  38.9 0.0 copy-done.3
  38.9 0.0 copy-done.4
  38.9 0.0 copy-done.5
  39.0 0.0 copy-done.6
  39.0 1.4 %filter_frames.1 = f32[32,32]{1,0:T(8,128)S(1)} custom-call(f32[32,128]{1,0:T(8,128)S(1)} %bitcast.19, f32[256,256]{1,0:T(8,128)S(1)} %copy-done.1, f32[1,128]{1,0:T(1,128)S(1)} %bitcast.21, f32[1,128]{1,0:T(1,128)S(1)} %bitcast.22, f32[1,128]{1,0:T(1,128)S(1)} %bitcast.23, f32[1,128]{1,0:T(1,128)S(1)} %bitcast.24, f32[256,256]{1,0:T(8,128)S(1)} %copy-done.2), custom_call_target="tpu_custom_call" | custom-call | tf_op jit(solution)/shard_map/filter_frames/pallas_call | solution.py:326
  40.4 15.3 %all_to_all.15 = f32[32,1,32]{2,1,0:T(1,128)S(1)} all-to-all(f32[32,1,32]{2,1,0:T(1,128)S(1)} %bitcast.20), channel_id=1, replica_groups=mesh['x'=4,'z'=16,'tile'=8] {'x','tile'}, dimensions={0} | all-to-all | bytes 8192 | tf_op jit(solution)/shard_map/all_to_all | solution.py:374
  55.6 0.6 reduce_sum.9
  (1 shorter events, 0.0 us)
Async XLA Ops:
  0.0 17.8 %copy-start = (bf16[2,16,128,256]{3,2,1,0:T(8,128)(2,1)S(1)}, bf16[2,16,128,256]{3,2,1,0:T(8,128)(2,1)}, u32[]{:S(2)}) copy-start(bf16[2,16,128,256]{3,2,1,0:T(8,128)(2,1)} %param.15) | copy-start | bytes 6291460
  1.8 12.8 %collective-permute-start = (bf16[3,128,128]{2,1,0:T(8,128)(2,1)S(1)}, bf16[3,128,128]{2,1,0:T(8,128)(2,1)S(1)}, u32[]{:S(2)}, u32[]{:S(2)}) collective-permute-start(bf16[3,128,128]{2,1,0:T(8,128)(2,1)S(1)} %get-tuple-element.19), channel_id=1, source_target_pairs={{0,1},{1,0},{2,3},{3,2},{4,5},{5,4},{6,7},{7,6},{8,9},{9,8},{10,11... | collective-permute-start | bytes 294920 | tf_op jit(solution)/shard_map/ppermute | solution.py:209
  10.6 5.9 %collective-permute-start.1 = (bf16[3,128,128]{2,1,0:T(8,128)(2,1)S(1)}, bf16[3,128,128]{2,1,0:T(8,128)(2,1)S(1)}, u32[]{:S(2)}, u32[]{:S(2)}) collective-permute-start(bf16[3,128,128]{2,1,0:T(8,128)(2,1)S(1)} %get-tuple-element.20), channel_id=1, source_target_pairs={{1,2},{3,4},{5,6},{2,1},{4,3},{6,5},{9,10},{11,12},{13,14},{10,9},... | collective-permute-start | bytes 294920 | tf_op jit(solution)/shard_map/ppermute | solution.py:208
  16.5 22.4 %copy-start.1 = (f32[256,256]{1,0:T(8,128)S(1)}, f32[256,256]{1,0:T(8,128)}, u32[]{:S(2)}) copy-start(f32[256,256]{1,0:T(8,128)} %input_ref.1) | copy-start | bytes 786436
  16.5 22.4 %copy-start.2 = (f32[256,256]{1,0:T(8,128)S(1)}, f32[256,256]{1,0:T(8,128)}, u32[]{:S(2)}) copy-start(f32[256,256]{1,0:T(8,128)} %readout_ref.1) | copy-start | bytes 786436
  16.5 22.4 %copy-start.3 = (f32[128]{0:T(128)S(1)}, f32[128]{0:T(128)}, u32[]{:S(2)}) copy-start(f32[128]{0:T(128)} %param.17) | copy-start | bytes 1540
  16.5 22.4 %copy-start.4 = (f32[128]{0:T(128)S(1)}, f32[128]{0:T(128)}, u32[]{:S(2)}) copy-start(f32[128]{0:T(128)} %param.18) | copy-start | bytes 1540
  16.5 22.4 %copy-start.5 = (f32[128]{0:T(128)S(1)}, f32[128]{0:T(128)}, u32[]{:S(2)}) copy-start(f32[128]{0:T(128)} %param.19) | copy-start | bytes 1540
  16.6 22.4 %copy-start.6 = (f32[128]{0:T(128)S(1)}, f32[128]{0:T(128)}, u32[]{:S(2)}) copy-start(f32[128]{0:T(128)} %param.20) | copy-start | bytes 1540

commit v5 on v4

--- a/solution.py
+++ b/solution.py
@@ -31,6 +31,15 @@
     ref[at, :PAD, :] = zeros
     ref[at, PAD : PAD + rows, :] = value.astype(ref.dtype)
     ref[at, PAD + rows :, :] = zeros
+
+
+def put_shifted(column, target):
+    half = target.shape[1]
+    for dr in range(3):
+        at = PAD - 1 + dr
+        target[dr] = jnp.concatenate(
+            [column[at : at + half, :], column[at + half : at + 2 * half, :]], axis=1
+        ).astype(target.dtype)
 
 
 def embed_kernel(frame_hbm, patch_hbm, depth_hbm, point_hbm, hidden_ref, partner_ref, other_ref, depth_ref,
@@ -125,32 +134,50 @@
     )(*(pltpu.with_memory_space_constraint(x, pltpu.HBM) for x in (frames, patch_weight, depth_weight, point_weight)))
 
 
-def taps_of(depth_ref, layer):
-    return [depth_ref[layer, k // 3, k % 3 : k % 3 + 1, :].astype(jnp.float32) for k in range(9)]
-
-
-def new_column(left, middle, right, taps, weight):
-    rows = middle.shape[0] - 2 * PAD
-    total = None
-    for dc, ref in enumerate((left, middle, right)):
-        for dr in range(3):
-            term = ref[PAD - 1 + dr : PAD - 1 + dr + rows, :] * taps[3 * dr + dc]
-            total = term if total is None else total + term
-    y = jnp.dot(total.astype(jnp.bfloat16), weight, preferred_element_type=jnp.float32)
-    return middle[PAD : PAD + rows, :] + gelu_of_half(y)
-
-
-def inner_kernel(hidden_ref, depth_ref, point_ref, one_ref, two_ref, sum_ref):
+def taps_of(depth_ref, layer, half):
+    channels = depth_ref.shape[3]
+    taps = []
+    for k in range(9):
+        tap = depth_ref[layer, k // 3, k % 3 : k % 3 + 1, :].astype(jnp.float32)
+        taps.append(jnp.broadcast_to(jnp.concatenate([tap, tap], axis=1), (half, 2 * channels)).astype(jnp.bfloat16))
+    return taps
+
+
+def weights_of(point_ref, layer):
+    weight = point_ref[layer].astype(jnp.float32) * 0.5
+    zero = jnp.zeros_like(weight)
+    return jnp.concatenate(
+        [jnp.concatenate([weight, zero], axis=1), jnp.concatenate([zero, weight], axis=1)], axis=0
+    ).astype(jnp.bfloat16)
+
+
+def new_column(left, middle, right, here, taps, weight):
+    half, channels = middle.shape[1], here.shape[1]
+    terms = [ref[dr] * taps[3 * dr + dc] for dc, ref in enumerate((left, middle, right)) for dr in range(3)]
+    while len(terms) > 1:
+        terms = [sum(terms[k : k + 2][1:], terms[k]) for k in range(0, len(terms), 2)]
+    y = gelu_of_half(jnp.dot(terms[0], weight, preferred_element_type=jnp.float32))
+    y = jnp.concatenate([y[:, :channels], y[:, channels:]], axis=0)
+    return here[PAD : PAD + 2 * half, :] + y
+
+
+def inner_kernel(hidden_ref, depth_ref, point_ref, one_ref, two_ref, sum_ref, shifted_ref):
     columns = hidden_ref.shape[0]
-    taps = [taps_of(depth_ref, layer) for layer in range(LAYERS)]
-    weights = [(point_ref[layer].astype(jnp.float32) * 0.5).astype(jnp.bfloat16) for layer in range(LAYERS)]
-    for layer, (source, target) in enumerate(((hidden_ref, one_ref), (one_ref, two_ref), (two_ref, None))):
+    rows = 2 * shifted_ref.shape[3]
+    taps = [taps_of(depth_ref, layer, rows // 2) for layer in range(LAYERS)]
+    weights = [weights_of(point_ref, layer) for layer in range(LAYERS)]
+    for at in range(columns):
+        put_shifted(hidden_ref.at[at], shifted_ref.at[0, at])
+    levels = (hidden_ref, one_ref, two_ref, None)
+    for layer in range(LAYERS):
+        source, target = levels[layer : layer + 2]
         for at in range(layer + 1, columns - layer - 1):
             value = new_column(
-                source.at[at - 1], source.at[at], source.at[at + 1], taps[layer], weights[layer]
+                *(shifted_ref.at[layer, at + dc] for dc in (-1, 0, 1)), source.at[at], taps[layer], weights[layer]
             )
             if target is not None:
                 put_column(target, at, value)
+                put_shifted(target.at[at], shifted_ref.at[layer + 1, at])
             elif at in (EDGE, columns // 2):
                 sum_ref[at // POOL] = value
             else:
@@ -158,33 +185,45 @@
 
 
 def outer_kernel(hidden_ref, one_ref, two_ref, sum_ref, partner_ref, other_ref, depth_ref, point_ref,
-                 pooled_ref, border_ref):
+                 pooled_ref, border_ref, shifted_ref):
     columns = hidden_ref.shape[0]
-    taps = [taps_of(depth_ref, layer) for layer in range(LAYERS)]
-    weights = [(point_ref[layer].astype(jnp.float32) * 0.5).astype(jnp.bfloat16) for layer in range(LAYERS)]
+    rows = 2 * shifted_ref.shape[4]
+    taps = [taps_of(depth_ref, layer, rows // 2) for layer in range(LAYERS)]
+    weights = [weights_of(point_ref, layer) for layer in range(LAYERS)]
     here, size = lax.axis_index("tile"), lax.axis_size("tile")
     odd = lax.rem(here, 2)
     inside = ((here > 0).astype(jnp.float32), (here < size - 1).astype(jnp.float32))
+    known = (hidden_ref, one_ref, two_ref)
+
+    def border(side, level, at):
+        return at + EDGE - level if side == 0 else at - columns + level
+
+    def shifted(side, level, at):
+        return shifted_ref.at[side, level, border(side, level, at) + (0 if side == 0 else 2)]
+
+    for level in range(LAYERS):
+        for at in (level, level + 1):
+            put_shifted(known[level].at[at], shifted(0, level, at))
+            mirror = columns - 1 - at
+            put_shifted(known[level].at[mirror], shifted(1, level, mirror))
     for halo, side in ((partner_ref, 1 - odd), (other_ref, odd)):
         for k in range(EDGE):
             put_column(border_ref.at[side, 0], k, halo[k].astype(jnp.float32))
-
-    def view(side, level, at):
-        if level <= at < columns - level:
-            return (hidden_ref, one_ref, two_ref)[level].at[at]
-        return border_ref.at[side, level, at + EDGE - level if side == 0 else at - columns + level]
+    for side in range(2):
+        for k in range(EDGE):
+            put_shifted(border_ref.at[side, 0, k], shifted_ref.at[side, 0, k + 2 * side])
 
     sums = [sum_ref[0], sum_ref[1]]
     for layer in range(LAYERS):
         for side in range(2):
             for k in range(EDGE):
                 at = k - 2 + layer if side == 0 else columns - 1 - layer + k
+                if layer <= at < columns - layer:
+                    source = known[layer].at[at]
+                else:
+                    source = border_ref.at[side, layer, border(side, layer, at)]
                 value = new_column(
-                    view(side, layer, at - 1),
-                    view(side, layer, at),
-                    view(side, layer, at + 1),
-                    taps[layer],
-                    weights[layer],
+                    *(shifted(side, layer, at + dc) for dc in (-1, 0, 1)), source, taps[layer], weights[layer]
                 )
                 if layer == LAYERS - 1:
                     sums[side] = sums[side] + value
@@ -192,7 +231,7 @@
                     if at < 0 or at >= columns:
                         value = value * inside[side]
                     put_column(border_ref.at[side, layer + 1], k, value)
-    rows = sums[0].shape[0]
+                    put_shifted(border_ref.at[side, layer + 1, k], shifted(side, layer + 1, at))
     for g in range(2):
         pooled_ref[g] = (
             jnp.sum(sums[g].reshape(rows // POOL, POOL, sums[g].shape[1]), axis=1) * (1.0 / (POOL * POOL))
@@ -207,7 +246,7 @@
     pairs = [(i, i + 1) for i in range(1, size - 1, 2)]
     other = lax.ppermute(other, "tile", pairs + [(j, i) for i, j in pairs])
     partner = lax.ppermute(partner, "tile", [(i, i ^ 1) for i in range(size)])
-    _, padded, channels = hidden.shape
+    columns, padded, channels = hidden.shape
     rows = padded - 2 * PAD
     level = jax.ShapeDtypeStruct(hidden.shape, jnp.float32)
     one, two, total = pl.pallas_call(
@@ -215,6 +254,7 @@
         out_shape=(level, level, jax.ShapeDtypeStruct((2, rows, channels), jnp.float32)),
         in_specs=[VMEM] * 3,
         out_specs=(VMEM,) * 3,
+        scratch_shapes=[pltpu.VMEM((LAYERS, columns, 3, rows // 2, 2 * channels), jnp.bfloat16)],
         compiler_params=pltpu.CompilerParams(vmem_limit_bytes=16 << 20),
         cost_estimate=pl.CostEstimate(flops=400_000_000, bytes_accessed=4_000_000, transcendentals=0),
         name="inner",
@@ -224,7 +264,10 @@
         out_shape=jax.ShapeDtypeStruct((2, rows // POOL, channels), jnp.bfloat16),
         in_specs=[VMEM] * 8,
         out_specs=VMEM,
-        scratch_shapes=[pltpu.VMEM((2, LAYERS, EDGE, padded, channels), jnp.float32)],
+        scratch_shapes=[
+            pltpu.VMEM((2, LAYERS, EDGE, padded, channels), jnp.float32),
+            pltpu.VMEM((2, LAYERS, EDGE + 2, 3, rows // 2, 2 * channels), jnp.bfloat16),
+        ],
         compiler_params=pltpu.CompilerParams(vmem_limit_bytes=20 << 20),
         name="outer",
     )(hidden, one, two, total, partner, other, depth_weight, point_weight)
@@ -300,7 +343,8 @@
     )
     length = lax.axis_size("z")
     mine = lax.rem(row, length) == lax.axis_index("z")
-    shares, width = out_ref.shape[0] // blocks, out_ref.shape[1]
+    shares = out_ref.shape[0] // blocks
+    width = readout_ref.shape[0] // shares
     real = jnp.sum(jnp.where(mine, real, 0.0).reshape(blocks, length, modes), axis=1)
     imag = jnp.sum(jnp.where(mine, imag, 0.0).reshape(blocks, length, modes), axis=1)
     if blocks < 8:
@@ -313,19 +357,18 @@
         jnp.where(is_real, lanes_at(real, mode + at), lanes_at(imag, mode + at)) for at in (0, modes // 2)
     ]
     latent = dot_t(jnp.concatenate(laid, axis=1), readout_ref[...])
-    share = lax.broadcasted_iota(jnp.int32, (shares, width), 0)
-    for block in range(blocks):
-        out = jnp.broadcast_to(latent[block : block + 1, :width], (shares, width))
-        for k in range(1, shares):
-            out = jnp.where(share == k, latent[block : block + 1, k * width : (k + 1) * width], out)
-        out_ref[block * shares : (block + 1) * shares, :] = out
+    lanes = out_ref.shape[1]
+    for k in range(shares):
+        at = k * width
+        half = latent[:, at // lanes * lanes : (at // lanes + 1) * lanes]
+        turn = (-at) % lanes
+        out_ref[pl.ds(k, blocks, stride=shares), :] = (pltpu.roll(half, turn, 1) if turn else half)[:blocks]
 
 
 def filter_frames(seen, input_map, mode_decay, mode_angle, smooth_decay, smooth_angle, readout, shares):
-    width = readout.shape[0] // shares
     return pl.pallas_call(
         filter_kernel,
-        out_shape=jax.ShapeDtypeStruct((lax.axis_size("x") * shares, width), jnp.float32),
+        out_shape=jax.ShapeDtypeStruct((lax.axis_size("x") * shares, seen.shape[1]), jnp.float32),
         in_specs=[VMEM] * 7,
         out_specs=VMEM,
         compiler_params=pltpu.CompilerParams(vmem_limit_bytes=8 << 20),
@@ -372,7 +415,7 @@
         seen, input_map, mode_decay, mode_angle, smooth_decay, smooth_angle, readout, tile_count
     )
     terms = lax.all_to_all(shares, ("x", "tile"), 0, 0)
-    return jnp.sum(terms, axis=0, keepdims=True)
+    return jnp.sum(terms, axis=0, keepdims=True)[:, : readout.shape[0] // tile_count]
 
 
 def solution(mesh):

time: 56.4 us -> 55.7 us (0.988)
  Pallas kernels: 6.52 us -> 5.37 us
  transfers between devices with their start and end apart: 2 -> 2, of which waited for: 1 -> 1; matrix products, arithmetic and copies ran while one was open for 0% -> 0% of each run, Pallas kernels for 4% -> 3%
where the time goes in v5:
time: 55.7 us; the launch traced here: 55.5 us
  blocking collectives  36 us (65%)
  starting transfers between devices  10.7 us (19%)
  Pallas kernels  5.37 us (10%)
  waiting for transfers between devices  2.36 us (4%)
  other arithmetic  0.56 us (1%)
    all_to_all x1, blocking collectives, shards(): lax.all_to_all(jnp.broadcast_to(partial_value.reshape(1, -1, 128), (lengt...  20.8 us
    all_to_all x1, blocking collectives, shards(): terms = lax.all_to_all(shares, ('x', 'tile'), 0, 0)  15.2 us
    ppermute x1, starting transfers between devices, encode(): partner = lax.ppermute(partner, 'tile', [(i, i ^ 1) for i in range(size)])  8.75 us
    ppermute x1, waiting for transfers between devices, encode(): other = lax.ppermute(other, 'tile', pairs + [(j, i) for i, j in pairs])  2.36 us
    ppermute x1, starting transfers between devices, encode(): other = lax.ppermute(other, 'tile', pairs + [(j, i) for i, j in pairs])  1.92 us
    pallas_call x1, Pallas kernels, embed(): pl.pallas_call(embed_kernel, out_shape=(jax.ShapeDtypeStruct((columns, ro...  1.83 us
    pallas_call x1, Pallas kernels, encode(): pl.pallas_call(inner_kernel, out_shape=(level, level, jax.ShapeDtypeStruc...  1.63 us
  transfers between devices with their start and end apart: 2, of which 1 were waited for; matrix products, arithmetic and copies ran while one was open for 0% of the time, Pallas kernels for 3%

profile of v5, /device:TPU:1, one launch (start us, length us, event | category | flops | bytes accessed | tf_op | source)
XLA Modules:
  0.0 55.5 jit_solution(6415601630150820323)
XLA Ops:
  0.0 0.0 copy-start
  0.0 1.8 %embed.1 = (f32[16,144,128]{2,1,0:T(8,128)S(1)}, bf16[3,128,128]{2,1,0:T(8,128)(2,1)S(1)}, bf16[3,128,128]{2,1,0:T(8,128)(2,1)S(1)}, bf16[3,3,3,128]{3,2,1,0:T(4,128)(2,1)S(1)}, bf16[3,128,128]{2,1,0:T(8,128)(2,1)S(1)}) custom-call(bf16[1,1024,128]{2,1,0:T(8,128)(2,1)} %frame_hbm.1, bf16[64,128]{1,0:T(8,128)(2,1)} %patch_hbm.1, ...), custom_call_target="tpu_custom_call" | custom-call | tf_op jit(solution)/shard_map/embed/pallas_call | solution.py:112
  1.8 8.7 %collective-permute-start = (bf16[3,128,128]{2,1,0:T(8,128)(2,1)S(1)}, bf16[3,128,128]{2,1,0:T(8,128)(2,1)S(1)}, u32[]{:S(2)}, u32[]{:S(2)}) collective-permute-start(bf16[3,128,128]{2,1,0:T(8,128)(2,1)S(1)} %get-tuple-element.19), channel_id=1, source_target_pairs={{0,1},{1,0},{2,3},{3,2},{4,5},{5,4},{6,7},{7,6},{8,9},{9,8},{10,11... | collective-permute-start | bytes 294920 | tf_op jit(solution)/shard_map/ppermute | solution.py:248
  10.6 1.9 %collective-permute-start.1 = (bf16[3,128,128]{2,1,0:T(8,128)(2,1)S(1)}, bf16[3,128,128]{2,1,0:T(8,128)(2,1)S(1)}, u32[]{:S(2)}, u32[]{:S(2)}) collective-permute-start(bf16[3,128,128]{2,1,0:T(8,128)(2,1)S(1)} %get-tuple-element.20), channel_id=1, source_target_pairs={{1,2},{3,4},{5,6},{2,1},{4,3},{6,5},{9,10},{11,12},{13,14},{10,9},... | collective-permute-start | bytes 294920 | tf_op jit(solution)/shard_map/ppermute | solution.py:247
  12.5 1.6 %inner.1 = (f32[16,144,128]{2,1,0:T(8,128)S(1)}, f32[16,144,128]{2,1,0:T(8,128)S(1)}, f32[2,128,128]{2,1,0:T(8,128)S(1)}) custom-call(f32[16,144,128]{2,1,0:T(8,128)S(1)} %get-tuple-element.13.hidden_ref, bf16[3,3,3,128]{3,2,1,0:T(4,128)(2,1)S(1)} %get-tuple-element.14.depth_ref, bf16[3,128,128]{2,1,0:T(8,128)(2,1)S(1)} %get-tuple-element.15.point_ref), custom_call_target="tpu_custom_call" | custom-call | flops 400000000 | bytes 4000000 | tf_op jit(solution)/shard_map/inner/pallas_call | solution.py:252
  14.2 0.0 collective-permute-done.partner_ref
  14.2 2.4 %collective-permute-done.1.other_ref = bf16[3,128,128]{2,1,0:T(8,128)(2,1)S(1)} collective-permute-done((bf16[3,128,128]{2,1,0:T(8,128)(2,1)S(1)}, bf16[3,128,128]{2,1,0:T(8,128)(2,1)S(1)}, u32[]{:S(2)}, u32[]{:S(2)}) %collective-permute-start.1) | collective-permute-done | bytes 98336 | tf_op jit(solution)/shard_map/ppermute | solution.py:247
  16.5 0.0 copy-start.1
  16.5 0.0 copy-start.2
  16.5 0.0 copy-start.3
  16.5 0.0 copy-start.4
  16.5 0.0 copy-start.5
  16.6 0.0 copy-start.6
  16.6 1.0 %outer.1 = bf16[2,16,128]{2,1,0:T(8,128)(2,1)S(1)} custom-call(f32[16,144,128]{2,1,0:T(8,128)S(1)} %get-tuple-element.13.hidden_ref, f32[16,144,128]{2,1,0:T(8,128)S(1)} %get-tuple-element.16.one_ref, f32[16,144,128]{2,1,0:T(8,128)S(1)} %get-tuple-element.17.two_ref, f32[2,128,128]{2,1,0:T(8,128)S(1)} %get-tuple-element.18.sum_ref, ...), custom_call_target="tpu_custom_call" | custom-call | tf_op jit(solution)/shard_map/outer/pallas_call | solution.py:262
  17.6 0.0 copy-done
  17.6 0.4 convolution_bitcast_fusion
  18.0 20.8 %all_to_all.14 = f32[16,2,128]{2,1,0:T(2,128)S(1)} all-to-all(f32[16,2,128]{2,1,0:T(2,128)S(1)} %broadcast_in_dim.23), channel_id=1, replica_groups=mesh['x'=4,'z'=16,'tile'=8] {'z'}, dimensions={0} | all-to-all | bytes 32768 | tf_op jit(solution)/shard_map/all_to_all | solution.py:408
  38.7 0.0 copy-done.1
  38.7 0.0 copy-done.2
  38.7 0.0 copy-done.3
  38.7 0.0 copy-done.4
  38.8 0.0 copy-done.5
  38.8 0.0 copy-done.6
  38.8 0.9 %filter_frames.1 = f32[32,128]{1,0:T(8,128)S(1)} custom-call(f32[32,128]{1,0:T(8,128)S(1)} %bitcast.20, f32[256,256]{1,0:T(8,128)S(1)} %copy-done.1, f32[1,128]{1,0:T(1,128)S(1)} %bitcast.22, f32[1,128]{1,0:T(1,128)S(1)} %bitcast.23, f32[1,128]{1,0:T(1,128)S(1)} %bitcast.24, f32[1,128]{1,0:T(1,128)S(1)} %bitcast.25, f32[256,256]{1,0:T(8,128)S(1)} %copy-done.2), custom_call_target="tpu_custom_call" | custom-call | tf_op jit(solution)/shard_map/filter_frames/pallas_call | solution.py:369
  39.7 15.2 %all_to_all.15 = f32[32,1,128]{2,1,0:T(1,128)S(1)} all-to-all(f32[32,1,128]{2,1,0:T(1,128)S(1)} %bitcast.21), channel_id=1, replica_groups=mesh['x'=4,'z'=16,'tile'=8] {'x','tile'}, dimensions={0} | all-to-all | bytes 32768 | tf_op jit(solution)/shard_map/all_to_all | solution.py:417
  54.9 0.6 %reduce_sum.9 = f32[128]{0:T(128)} reduce(f32[32,1,128]{2,1,0:T(1,128)S(1)} %all_to_all.15, f32[]{:T(128)} %constant.0.clone.1), dimensions={0,1}, to_apply=%region_0.0 | reduce | flops 3968 | bytes 16900 | tf_op jit(solution)/shard_map/reduce_sum | solution.py:418
  (1 shorter events, 0.0 us)
Async XLA Ops:
  0.0 17.6 %copy-start = (bf16[2,16,128,256]{3,2,1,0:T(8,128)(2,1)S(1)}, bf16[2,16,128,256]{3,2,1,0:T(8,128)(2,1)}, u32[]{:S(2)}) copy-start(bf16[2,16,128,256]{3,2,1,0:T(8,128)(2,1)} %param.15) | copy-start | bytes 6291460
  1.8 12.3 %collective-permute-start = (bf16[3,128,128]{2,1,0:T(8,128)(2,1)S(1)}, bf16[3,128,128]{2,1,0:T(8,128)(2,1)S(1)}, u32[]{:S(2)}, u32[]{:S(2)}) collective-permute-start(bf16[3,128,128]{2,1,0:T(8,128)(2,1)S(1)} %get-tuple-element.19), channel_id=1, source_target_pairs={{0,1},{1,0},{2,3},{3,2},{4,5},{5,4},{6,7},{7,6},{8,9},{9,8},{10,11... | collective-permute-start | bytes 294920 | tf_op jit(solution)/shard_map/ppermute | solution.py:248
  10.6 5.9 %collective-permute-start.1 = (bf16[3,128,128]{2,1,0:T(8,128)(2,1)S(1)}, bf16[3,128,128]{2,1,0:T(8,128)(2,1)S(1)}, u32[]{:S(2)}, u32[]{:S(2)}) collective-permute-start(bf16[3,128,128]{2,1,0:T(8,128)(2,1)S(1)} %get-tuple-element.20), channel_id=1, source_target_pairs={{1,2},{3,4},{5,6},{2,1},{4,3},{6,5},{9,10},{11,12},{13,14},{10,9},... | collective-permute-start | bytes 294920 | tf_op jit(solution)/shard_map/ppermute | solution.py:247
  16.5 22.2 %copy-start.1 = (f32[256,256]{1,0:T(8,128)S(1)}, f32[256,256]{1,0:T(8,128)}, u32[]{:S(2)}) copy-start(f32[256,256]{1,0:T(8,128)} %input_ref.1) | copy-start | bytes 786436
  16.5 22.2 %copy-start.2 = (f32[256,256]{1,0:T(8,128)S(1)}, f32[256,256]{1,0:T(8,128)}, u32[]{:S(2)}) copy-start(f32[256,256]{1,0:T(8,128)} %readout_ref.1) | copy-start | bytes 786436
  16.5 22.2 %copy-start.3 = (f32[128]{0:T(128)S(1)}, f32[128]{0:T(128)}, u32[]{:S(2)}) copy-start(f32[128]{0:T(128)} %param.17) | copy-start | bytes 1540
  16.5 22.2 %copy-start.4 = (f32[128]{0:T(128)S(1)}, f32[128]{0:T(128)}, u32[]{:S(2)}) copy-start(f32[128]{0:T(128)} %param.18) | copy-start | bytes 1540
  16.5 22.2 %copy-start.5 = (f32[128]{0:T(128)S(1)}, f32[128]{0:T(128)}, u32[]{:S(2)}) copy-start(f32[128]{0:T(128)} %param.19) | copy-start | bytes 1540
  16.6 22.2 %copy-start.6 = (f32[128]{0:T(128)S(1)}, f32[128]{0:T(128)}, u32[]{:S(2)}) copy-start(f32[128]{0:T(128)} %param.20) | copy-start | bytes 1540

commit v6 on v5

--- a/solution.py
+++ b/solution.py
@@ -10,6 +10,10 @@
 POOL = 8
 LAYERS = 3
 BLOCKS = 4
+
+
+def from_middle(size):
+    return [(i + size // 2) % size for i in range(size)]
 
 
 PAD = 8
@@ -328,6 +332,7 @@
     in_lower = lane < modes // 2
     real = jnp.where(in_lower, lanes_at(lower, even), lanes_at(upper, even)) * gain
     imag = jnp.where(in_lower, lanes_at(lower, even + 1), lanes_at(upper, even + 1)) * gain
+    real, imag = (pltpu.roll(part, frames // 2, 0) for part in (real, imag))
     blocks = lax.axis_size("x")
     row = lax.broadcasted_iota(jnp.int32, (blocks * frames, modes), 0)
     placed = row // frames == lax.axis_index("x")
@@ -362,7 +367,9 @@
         at = k * width
         half = latent[:, at // lanes * lanes : (at // lanes + 1) * lanes]
         turn = (-at) % lanes
-        out_ref[pl.ds(k, blocks, stride=shares), :] = (pltpu.roll(half, turn, 1) if turn else half)[:blocks]
+        half = pltpu.roll(half, turn, 1) if turn else half
+        place = (k + shares - shares // 2) % shares
+        out_ref[pl.ds(place, blocks, stride=shares), :] = half[blocks // 2 : blocks // 2 + blocks]
 
 
 def filter_frames(seen, input_map, mode_decay, mode_angle, smooth_decay, smooth_angle, readout, shares):
@@ -410,11 +417,15 @@
         "z",
         0,
         0,
+        axis_index_groups=[from_middle(length)],
     ).reshape(-1, 128)
     shares = filter_frames(
         seen, input_map, mode_decay, mode_angle, smooth_decay, smooth_angle, readout, tile_count
     )
-    terms = lax.all_to_all(shares, ("x", "tile"), 0, 0)
+    order = [
+        x * tile_count + tile for x in from_middle(lax.axis_size("x")) for tile in from_middle(tile_count)
+    ]
+    terms = lax.all_to_all(shares, ("x", "tile"), 0, 0, axis_index_groups=[order])
     return jnp.sum(terms, axis=0, keepdims=True)[:, : readout.shape[0] // tile_count]
 
 

time: 55.7 us -> 46.1 us (0.83)
  blocking collectives: 36 us -> 26.4 us
    all_to_all x1, blocking collectives: 20.8 us -> 14.5 us  [shards(): lax.all_to_all(jnp.broadcast_to(partial_value.reshape(1, -1, 128), (lengt...]
    all_to_all x1, blocking collectives: 15.2 us -> 11.9 us  [shards(): lax.all_to_all(shares, ('x', 'tile'), 0, 0, axis_index_groups=[order])]
  transfers between devices with their start and end apart: 2 -> 2, of which waited for: 1 -> 1; matrix products, arithmetic and copies ran while one was open for 0% -> 0% of each run, Pallas kernels for 3% -> 4%
where the time goes in v6:
time: 46.1 us; the launch traced here: 45.9 us
  blocking collectives  26.4 us (57%)
  starting transfers between devices  10.7 us (23%)
  Pallas kernels  5.38 us (12%)
  waiting for transfers between devices  2.36 us (5%)
  other arithmetic  0.56 us (1%)
    all_to_all x1, blocking collectives, shards(): lax.all_to_all(jnp.broadcast_to(partial_value.reshape(1, -1, 128), (lengt...  14.5 us
    all_to_all x1, blocking collectives, shards(): lax.all_to_all(shares, ('x', 'tile'), 0, 0, axis_index_groups=[order])  11.9 us
    ppermute x1, starting transfers between devices, encode(): partner = lax.ppermute(partner, 'tile', [(i, i ^ 1) for i in range(size)])  8.75 us
    ppermute x1, waiting for transfers between devices, encode(): other = lax.ppermute(other, 'tile', pairs + [(j, i) for i, j in pairs])  2.36 us
    ppermute x1, starting transfers between devices, encode(): other = lax.ppermute(other, 'tile', pairs + [(j, i) for i, j in pairs])  1.92 us
    pallas_call x1, Pallas kernels, embed(): pl.pallas_call(embed_kernel, out_shape=(jax.ShapeDtypeStruct((columns, ro...  1.83 us
    pallas_call x1, Pallas kernels, encode(): pl.pallas_call(inner_kernel, out_shape=(level, level, jax.ShapeDtypeStruc...  1.63 us
    pallas_call x1, Pallas kernels, encode(): pl.pallas_call(outer_kernel, out_shape=jax.ShapeDtypeStruct((2, rows // P...  1 us
  transfers between devices with their start and end apart: 2, of which 1 were waited for; matrix products, arithmetic and copies ran while one was open for 0% of the time, Pallas kernels for 4%

profile of v6, /device:TPU:1, one launch (start us, length us, event | category | flops | bytes accessed | tf_op | source)
XLA Modules:
  0.0 45.9 jit_solution(9415478271666492348)
XLA Ops:
  0.0 0.0 copy-start
  0.0 1.8 %embed.1 = (f32[16,144,128]{2,1,0:T(8,128)S(1)}, bf16[3,128,128]{2,1,0:T(8,128)(2,1)S(1)}, bf16[3,128,128]{2,1,0:T(8,128)(2,1)S(1)}, bf16[3,3,3,128]{3,2,1,0:T(4,128)(2,1)S(1)}, bf16[3,128,128]{2,1,0:T(8,128)(2,1)S(1)}) custom-call(bf16[1,1024,128]{2,1,0:T(8,128)(2,1)} %frame_hbm.1, bf16[64,128]{1,0:T(8,128)(2,1)} %patch_hbm.1, ...), custom_call_target="tpu_custom_call" | custom-call | tf_op jit(solution)/shard_map/embed/pallas_call | solution.py:116
  1.8 8.7 %collective-permute-start = (bf16[3,128,128]{2,1,0:T(8,128)(2,1)S(1)}, bf16[3,128,128]{2,1,0:T(8,128)(2,1)S(1)}, u32[]{:S(2)}, u32[]{:S(2)}) collective-permute-start(bf16[3,128,128]{2,1,0:T(8,128)(2,1)S(1)} %get-tuple-element.19), channel_id=1, source_target_pairs={{0,1},{1,0},{2,3},{3,2},{4,5},{5,4},{6,7},{7,6},{8,9},{9,8},{10,11... | collective-permute-start | bytes 294920 | tf_op jit(solution)/shard_map/ppermute | solution.py:252
  10.6 1.9 %collective-permute-start.1 = (bf16[3,128,128]{2,1,0:T(8,128)(2,1)S(1)}, bf16[3,128,128]{2,1,0:T(8,128)(2,1)S(1)}, u32[]{:S(2)}, u32[]{:S(2)}) collective-permute-start(bf16[3,128,128]{2,1,0:T(8,128)(2,1)S(1)} %get-tuple-element.20), channel_id=1, source_target_pairs={{1,2},{3,4},{5,6},{2,1},{4,3},{6,5},{9,10},{11,12},{13,14},{10,9},... | collective-permute-start | bytes 294920 | tf_op jit(solution)/shard_map/ppermute | solution.py:251
  12.5 1.6 %inner.1 = (f32[16,144,128]{2,1,0:T(8,128)S(1)}, f32[16,144,128]{2,1,0:T(8,128)S(1)}, f32[2,128,128]{2,1,0:T(8,128)S(1)}) custom-call(f32[16,144,128]{2,1,0:T(8,128)S(1)} %get-tuple-element.13.hidden_ref, bf16[3,3,3,128]{3,2,1,0:T(4,128)(2,1)S(1)} %get-tuple-element.14.depth_ref, bf16[3,128,128]{2,1,0:T(8,128)(2,1)S(1)} %get-tuple-element.15.point_ref), custom_call_target="tpu_custom_call" | custom-call | flops 400000000 | bytes 4000000 | tf_op jit(solution)/shard_map/inner/pallas_call | solution.py:256
  14.2 0.0 collective-permute-done.partner_ref
  14.2 2.4 %collective-permute-done.1.other_ref = bf16[3,128,128]{2,1,0:T(8,128)(2,1)S(1)} collective-permute-done((bf16[3,128,128]{2,1,0:T(8,128)(2,1)S(1)}, bf16[3,128,128]{2,1,0:T(8,128)(2,1)S(1)}, u32[]{:S(2)}, u32[]{:S(2)}) %collective-permute-start.1) | collective-permute-done | bytes 98336 | tf_op jit(solution)/shard_map/ppermute | solution.py:251
  16.5 0.0 copy-start.1
  16.5 0.0 copy-start.2
  16.5 0.0 copy-start.3
  16.5 0.0 copy-start.4
  16.5 0.0 copy-start.5
  16.6 0.0 copy-start.6
  16.6 1.0 %outer.1 = bf16[2,16,128]{2,1,0:T(8,128)(2,1)S(1)} custom-call(f32[16,144,128]{2,1,0:T(8,128)S(1)} %get-tuple-element.13.hidden_ref, f32[16,144,128]{2,1,0:T(8,128)S(1)} %get-tuple-element.16.one_ref, f32[16,144,128]{2,1,0:T(8,128)S(1)} %get-tuple-element.17.two_ref, f32[2,128,128]{2,1,0:T(8,128)S(1)} %get-tuple-element.18.sum_ref, ...), custom_call_target="tpu_custom_call" | custom-call | tf_op jit(solution)/shard_map/outer/pallas_call | solution.py:266
  17.6 0.0 copy-done
  17.6 0.4 convolution_bitcast_fusion
  18.0 14.5 %all_to_all.14 = f32[16,2,128]{2,1,0:T(2,128)S(1)} all-to-all(f32[16,2,128]{2,1,0:T(2,128)S(1)} %broadcast_in_dim.23), channel_id=1, replica_groups={{64,72,80,88,96,104,112,120,0,8,16,24,32,40,48,56},{65,73,81,89,97,105,..., dimensions={0} | all-to-all | bytes 32768 | tf_op jit(solution)/shard_map/all_to_all | solution.py:415
  32.5 0.0 copy-done.1
  32.5 0.0 copy-done.2
  32.5 0.0 copy-done.3
  32.5 0.0 copy-done.4
  32.5 0.0 copy-done.5
  32.5 0.0 copy-done.6
  32.5 0.9 %filter_frames.1 = f32[32,128]{1,0:T(8,128)S(1)} custom-call(f32[32,128]{1,0:T(8,128)S(1)} %bitcast.20, f32[256,256]{1,0:T(8,128)S(1)} %copy-done.1, f32[1,128]{1,0:T(1,128)S(1)} %bitcast.22, f32[1,128]{1,0:T(1,128)S(1)} %bitcast.23, f32[1,128]{1,0:T(1,128)S(1)} %bitcast.24, f32[1,128]{1,0:T(1,128)S(1)} %bitcast.25, f32[256,256]{1,0:T(8,128)S(1)} %copy-done.2), custom_call_target="tpu_custom_call" | custom-call | tf_op jit(solution)/shard_map/filter_frames/pallas_call | solution.py:376
  33.4 11.9 %all_to_all.15 = f32[32,1,128]{2,1,0:T(1,128)S(1)} all-to-all(f32[32,1,128]{2,1,0:T(1,128)S(1)} %bitcast.21), channel_id=1, replica_groups={{260,261,262,263,256,257,258,259,388,389,390,391,384,385,386,387,4,5,6,..., dimensions={0} | all-to-all | bytes 32768 | tf_op jit(solution)/shard_map/all_to_all | solution.py:428
  45.3 0.6 %reduce_sum.9 = f32[128]{0:T(128)} reduce(f32[32,1,128]{2,1,0:T(1,128)S(1)} %all_to_all.15, f32[]{:T(128)} %constant.0.clone.1), dimensions={0,1}, to_apply=%region_0.0 | reduce | flops 3968 | bytes 16900 | tf_op jit(solution)/shard_map/reduce_sum | solution.py:429
  (1 shorter events, 0.0 us)
Async XLA Ops:
  0.0 17.6 %copy-start = (bf16[2,16,128,256]{3,2,1,0:T(8,128)(2,1)S(1)}, bf16[2,16,128,256]{3,2,1,0:T(8,128)(2,1)}, u32[]{:S(2)}) copy-start(bf16[2,16,128,256]{3,2,1,0:T(8,128)(2,1)} %param.15) | copy-start | bytes 6291460
  1.8 12.3 %collective-permute-start = (bf16[3,128,128]{2,1,0:T(8,128)(2,1)S(1)}, bf16[3,128,128]{2,1,0:T(8,128)(2,1)S(1)}, u32[]{:S(2)}, u32[]{:S(2)}) collective-permute-start(bf16[3,128,128]{2,1,0:T(8,128)(2,1)S(1)} %get-tuple-element.19), channel_id=1, source_target_pairs={{0,1},{1,0},{2,3},{3,2},{4,5},{5,4},{6,7},{7,6},{8,9},{9,8},{10,11... | collective-permute-start | bytes 294920 | tf_op jit(solution)/shard_map/ppermute | solution.py:252
  10.6 5.9 %collective-permute-start.1 = (bf16[3,128,128]{2,1,0:T(8,128)(2,1)S(1)}, bf16[3,128,128]{2,1,0:T(8,128)(2,1)S(1)}, u32[]{:S(2)}, u32[]{:S(2)}) collective-permute-start(bf16[3,128,128]{2,1,0:T(8,128)(2,1)S(1)} %get-tuple-element.20), channel_id=1, source_target_pairs={{1,2},{3,4},{5,6},{2,1},{4,3},{6,5},{9,10},{11,12},{13,14},{10,9},... | collective-permute-start | bytes 294920 | tf_op jit(solution)/shard_map/ppermute | solution.py:251
  16.5 15.9 %copy-start.1 = (f32[256,256]{1,0:T(8,128)S(1)}, f32[256,256]{1,0:T(8,128)}, u32[]{:S(2)}) copy-start(f32[256,256]{1,0:T(8,128)} %input_ref.1) | copy-start | bytes 786436
  16.5 15.9 %copy-start.2 = (f32[256,256]{1,0:T(8,128)S(1)}, f32[256,256]{1,0:T(8,128)}, u32[]{:S(2)}) copy-start(f32[256,256]{1,0:T(8,128)} %readout_ref.1) | copy-start | bytes 786436
  16.5 15.9 %copy-start.3 = (f32[128]{0:T(128)S(1)}, f32[128]{0:T(128)}, u32[]{:S(2)}) copy-start(f32[128]{0:T(128)} %param.17) | copy-start | bytes 1540
  16.5 15.9 %copy-start.4 = (f32[128]{0:T(128)S(1)}, f32[128]{0:T(128)}, u32[]{:S(2)}) copy-start(f32[128]{0:T(128)} %param.18) | copy-start | bytes 1540
  16.5 16.0 %copy-start.5 = (f32[128]{0:T(128)S(1)}, f32[128]{0:T(128)}, u32[]{:S(2)}) copy-start(f32[128]{0:T(128)} %param.19) | copy-start | bytes 1540
  16.6 16.0 %copy-start.6 = (f32[128]{0:T(128)S(1)}, f32[128]{0:T(128)}, u32[]{:S(2)}) copy-start(f32[128]{0:T(128)} %param.20) | copy-start | bytes 1540

commit v7 on v5

--- a/solution.py
+++ b/solution.py
@@ -10,6 +10,14 @@
 POOL = 8
 LAYERS = 3
 BLOCKS = 4
+
+
+def led_by(size, first):
+    return [first] + [i for i in range(size) if i != first]
+
+
+def middle_of(blocks, shares):
+    return blocks // 2 * shares + shares // 2
 
 
 PAD = 8
@@ -328,6 +336,13 @@
     in_lower = lane < modes // 2
     real = jnp.where(in_lower, lanes_at(lower, even), lanes_at(upper, even)) * gain
     imag = jnp.where(in_lower, lanes_at(lower, even + 1), lanes_at(upper, even + 1)) * gain
+    arrived = lax.broadcasted_iota(jnp.int32, real.shape, 0)
+
+    def in_order(part):
+        others = jnp.where(arrived < frames // 2, pltpu.roll(part, frames - 1, 0), part)
+        return jnp.where(arrived == frames // 2, jnp.broadcast_to(part[:1], part.shape), others)
+
+    real, imag = in_order(real), in_order(imag)
     blocks = lax.axis_size("x")
     row = lax.broadcasted_iota(jnp.int32, (blocks * frames, modes), 0)
     placed = row // frames == lax.axis_index("x")
@@ -363,6 +378,11 @@
         half = latent[:, at // lanes * lanes : (at // lanes + 1) * lanes]
         turn = (-at) % lanes
         out_ref[pl.ds(k, blocks, stride=shares), :] = (pltpu.roll(half, turn, 1) if turn else half)[:blocks]
+    out = out_ref[...]
+    first = middle_of(blocks, shares)
+    place = lax.broadcasted_iota(jnp.int32, out.shape, 0)
+    others = jnp.where(place <= first, pltpu.roll(out, 1, 0), out)
+    out_ref[...] = jnp.where(place == 0, jnp.broadcast_to(out[first : first + 1], out.shape), others)
 
 
 def filter_frames(seen, input_map, mode_decay, mode_angle, smooth_decay, smooth_angle, readout, shares):
@@ -410,11 +430,14 @@
         "z",
         0,
         0,
+        axis_index_groups=[led_by(length, length // 2)],
     ).reshape(-1, 128)
     shares = filter_frames(
         seen, input_map, mode_decay, mode_angle, smooth_decay, smooth_angle, readout, tile_count
     )
-    terms = lax.all_to_all(shares, ("x", "tile"), 0, 0)
+    blocks = lax.axis_size("x")
+    order = led_by(blocks * tile_count, middle_of(blocks, tile_count))
+    terms = lax.all_to_all(shares, ("x", "tile"), 0, 0, axis_index_groups=[order])
     return jnp.sum(terms, axis=0, keepdims=True)[:, : readout.shape[0] // tile_count]
 
 

time: 55.7 us -> 46.1 us (0.83)
  blocking collectives: 36 us -> 26.4 us
    all_to_all x1, blocking collectives: 20.8 us -> 14.5 us  [shards(): lax.all_to_all(jnp.broadcast_to(partial_value.reshape(1, -1, 128), (lengt...]
    all_to_all x1, blocking collectives: 15.2 us -> 11.9 us  [shards(): lax.all_to_all(shares, ('x', 'tile'), 0, 0, axis_index_groups=[order])]
  transfers between devices with their start and end apart: 2 -> 2, of which waited for: 1 -> 1; matrix products, arithmetic and copies ran while one was open for 0% -> 0% of each run, Pallas kernels for 3% -> 4%
where the time goes in v7:
time: 46.1 us; the launch traced here: 45.9 us
  blocking collectives  26.4 us (57%)
  starting transfers between devices  10.7 us (23%)
  Pallas kernels  5.39 us (12%)
  waiting for transfers between devices  2.36 us (5%)
  other arithmetic  0.56 us (1%)
    all_to_all x1, blocking collectives, shards(): lax.all_to_all(jnp.broadcast_to(partial_value.reshape(1, -1, 128), (lengt...  14.5 us
    all_to_all x1, blocking collectives, shards(): lax.all_to_all(shares, ('x', 'tile'), 0, 0, axis_index_groups=[order])  11.9 us
    ppermute x1, starting transfers between devices, encode(): partner = lax.ppermute(partner, 'tile', [(i, i ^ 1) for i in range(size)])  8.75 us
    ppermute x1, waiting for transfers between devices, encode(): other = lax.ppermute(other, 'tile', pairs + [(j, i) for i, j in pairs])  2.36 us
    ppermute x1, starting transfers between devices, encode(): other = lax.ppermute(other, 'tile', pairs + [(j, i) for i, j in pairs])  1.92 us
    pallas_call x1, Pallas kernels, embed(): pl.pallas_call(embed_kernel, out_shape=(jax.ShapeDtypeStruct((columns, ro...  1.83 us
    pallas_call x1, Pallas kernels, encode(): pl.pallas_call(inner_kernel, out_shape=(level, level, jax.ShapeDtypeStruc...  1.63 us
    pallas_call x1, Pallas kernels, encode(): pl.pallas_call(outer_kernel, out_shape=jax.ShapeDtypeStruct((2, rows // P...  1 us
  transfers between devices with their start and end apart: 2, of which 1 were waited for; matrix products, arithmetic and copies ran while one was open for 0% of the time, Pallas kernels for 4%

profile of v7, /device:TPU:1, one launch (start us, length us, event | category | flops | bytes accessed | tf_op | source)
XLA Modules:
  0.0 45.9 jit_solution(18408084431256077368)
XLA Ops:
  0.0 0.0 copy-start
  0.0 1.8 %embed.1 = (f32[16,144,128]{2,1,0:T(8,128)S(1)}, bf16[3,128,128]{2,1,0:T(8,128)(2,1)S(1)}, bf16[3,128,128]{2,1,0:T(8,128)(2,1)S(1)}, bf16[3,3,3,128]{3,2,1,0:T(4,128)(2,1)S(1)}, bf16[3,128,128]{2,1,0:T(8,128)(2,1)S(1)}) custom-call(bf16[1,1024,128]{2,1,0:T(8,128)(2,1)} %frame_hbm.1, bf16[64,128]{1,0:T(8,128)(2,1)} %patch_hbm.1, ...), custom_call_target="tpu_custom_call" | custom-call | tf_op jit(solution)/shard_map/embed/pallas_call | solution.py:120
  1.8 8.7 %collective-permute-start = (bf16[3,128,128]{2,1,0:T(8,128)(2,1)S(1)}, bf16[3,128,128]{2,1,0:T(8,128)(2,1)S(1)}, u32[]{:S(2)}, u32[]{:S(2)}) collective-permute-start(bf16[3,128,128]{2,1,0:T(8,128)(2,1)S(1)} %get-tuple-element.19), channel_id=1, source_target_pairs={{0,1},{1,0},{2,3},{3,2},{4,5},{5,4},{6,7},{7,6},{8,9},{9,8},{10,11... | collective-permute-start | bytes 294920 | tf_op jit(solution)/shard_map/ppermute | solution.py:256
  10.6 1.9 %collective-permute-start.1 = (bf16[3,128,128]{2,1,0:T(8,128)(2,1)S(1)}, bf16[3,128,128]{2,1,0:T(8,128)(2,1)S(1)}, u32[]{:S(2)}, u32[]{:S(2)}) collective-permute-start(bf16[3,128,128]{2,1,0:T(8,128)(2,1)S(1)} %get-tuple-element.20), channel_id=1, source_target_pairs={{1,2},{3,4},{5,6},{2,1},{4,3},{6,5},{9,10},{11,12},{13,14},{10,9},... | collective-permute-start | bytes 294920 | tf_op jit(solution)/shard_map/ppermute | solution.py:255
  12.5 1.6 %inner.1 = (f32[16,144,128]{2,1,0:T(8,128)S(1)}, f32[16,144,128]{2,1,0:T(8,128)S(1)}, f32[2,128,128]{2,1,0:T(8,128)S(1)}) custom-call(f32[16,144,128]{2,1,0:T(8,128)S(1)} %get-tuple-element.13.hidden_ref, bf16[3,3,3,128]{3,2,1,0:T(4,128)(2,1)S(1)} %get-tuple-element.14.depth_ref, bf16[3,128,128]{2,1,0:T(8,128)(2,1)S(1)} %get-tuple-element.15.point_ref), custom_call_target="tpu_custom_call" | custom-call | flops 400000000 | bytes 4000000 | tf_op jit(solution)/shard_map/inner/pallas_call | solution.py:260
  14.2 0.0 collective-permute-done.partner_ref
  14.2 2.4 %collective-permute-done.1.other_ref = bf16[3,128,128]{2,1,0:T(8,128)(2,1)S(1)} collective-permute-done((bf16[3,128,128]{2,1,0:T(8,128)(2,1)S(1)}, bf16[3,128,128]{2,1,0:T(8,128)(2,1)S(1)}, u32[]{:S(2)}, u32[]{:S(2)}) %collective-permute-start.1) | collective-permute-done | bytes 98336 | tf_op jit(solution)/shard_map/ppermute | solution.py:255
  16.5 0.0 copy-start.1
  16.5 0.0 copy-start.2
  16.5 0.0 copy-start.3
  16.5 0.0 copy-start.4
  16.5 0.0 copy-start.5
  16.6 0.0 copy-start.6
  16.6 1.0 %outer.1 = bf16[2,16,128]{2,1,0:T(8,128)(2,1)S(1)} custom-call(f32[16,144,128]{2,1,0:T(8,128)S(1)} %get-tuple-element.13.hidden_ref, f32[16,144,128]{2,1,0:T(8,128)S(1)} %get-tuple-element.16.one_ref, f32[16,144,128]{2,1,0:T(8,128)S(1)} %get-tuple-element.17.two_ref, f32[2,128,128]{2,1,0:T(8,128)S(1)} %get-tuple-element.18.sum_ref, ...), custom_call_target="tpu_custom_call" | custom-call | tf_op jit(solution)/shard_map/outer/pallas_call | solution.py:270
  17.6 0.0 copy-done
  17.6 0.4 convolution_bitcast_fusion
  18.0 14.5 %all_to_all.14 = f32[16,2,128]{2,1,0:T(2,128)S(1)} all-to-all(f32[16,2,128]{2,1,0:T(2,128)S(1)} %broadcast_in_dim.23), channel_id=1, replica_groups={{64,0,8,16,24,32,40,48,56,72,80,88,96,104,112,120},{65,1,9,17,25,33,41,..., dimensions={0} | all-to-all | bytes 32768 | tf_op jit(solution)/shard_map/all_to_all | solution.py:428
  32.5 0.0 copy-done.1
  32.5 0.0 copy-done.2
  32.5 0.0 copy-done.3
  32.5 0.0 copy-done.4
  32.5 0.0 copy-done.5
  32.5 0.0 copy-done.6
  32.5 0.9 %filter_frames.1 = f32[32,128]{1,0:T(8,128)S(1)} custom-call(f32[32,128]{1,0:T(8,128)S(1)} %bitcast.20, f32[256,256]{1,0:T(8,128)S(1)} %copy-done.1, f32[1,128]{1,0:T(1,128)S(1)} %bitcast.22, f32[1,128]{1,0:T(1,128)S(1)} %bitcast.23, f32[1,128]{1,0:T(1,128)S(1)} %bitcast.24, f32[1,128]{1,0:T(1,128)S(1)} %bitcast.25, f32[256,256]{1,0:T(8,128)S(1)} %copy-done.2), custom_call_target="tpu_custom_call" | custom-call | tf_op jit(solution)/shard_map/filter_frames/pallas_call | solution.py:389
  33.4 11.9 %all_to_all.15 = f32[32,1,128]{2,1,0:T(1,128)S(1)} all-to-all(f32[32,1,128]{2,1,0:T(1,128)S(1)} %bitcast.21), channel_id=1, replica_groups={{260,0,1,2,3,4,5,6,7,128,129,130,131,132,133,134,135,256,257,258,259,26..., dimensions={0} | all-to-all | bytes 32768 | tf_op jit(solution)/shard_map/all_to_all | solution.py:440
  45.3 0.6 %reduce_sum.9 = f32[128]{0:T(128)} reduce(f32[32,1,128]{2,1,0:T(1,128)S(1)} %all_to_all.15, f32[]{:T(128)} %constant.0.clone.1), dimensions={0,1}, to_apply=%region_0.0 | reduce | flops 3968 | bytes 16900 | tf_op jit(solution)/shard_map/reduce_sum | solution.py:441
  (1 shorter events, 0.0 us)
Async XLA Ops:
  0.0 17.6 %copy-start = (bf16[2,16,128,256]{3,2,1,0:T(8,128)(2,1)S(1)}, bf16[2,16,128,256]{3,2,1,0:T(8,128)(2,1)}, u32[]{:S(2)}) copy-start(bf16[2,16,128,256]{3,2,1,0:T(8,128)(2,1)} %param.15) | copy-start | bytes 6291460
  1.8 12.3 %collective-permute-start = (bf16[3,128,128]{2,1,0:T(8,128)(2,1)S(1)}, bf16[3,128,128]{2,1,0:T(8,128)(2,1)S(1)}, u32[]{:S(2)}, u32[]{:S(2)}) collective-permute-start(bf16[3,128,128]{2,1,0:T(8,128)(2,1)S(1)} %get-tuple-element.19), channel_id=1, source_target_pairs={{0,1},{1,0},{2,3},{3,2},{4,5},{5,4},{6,7},{7,6},{8,9},{9,8},{10,11... | collective-permute-start | bytes 294920 | tf_op jit(solution)/shard_map/ppermute | solution.py:256
  10.6 5.9 %collective-permute-start.1 = (bf16[3,128,128]{2,1,0:T(8,128)(2,1)S(1)}, bf16[3,128,128]{2,1,0:T(8,128)(2,1)S(1)}, u32[]{:S(2)}, u32[]{:S(2)}) collective-permute-start(bf16[3,128,128]{2,1,0:T(8,128)(2,1)S(1)} %get-tuple-element.20), channel_id=1, source_target_pairs={{1,2},{3,4},{5,6},{2,1},{4,3},{6,5},{9,10},{11,12},{13,14},{10,9},... | collective-permute-start | bytes 294920 | tf_op jit(solution)/shard_map/ppermute | solution.py:255
  16.5 15.9 %copy-start.1 = (f32[256,256]{1,0:T(8,128)S(1)}, f32[256,256]{1,0:T(8,128)}, u32[]{:S(2)}) copy-start(f32[256,256]{1,0:T(8,128)} %input_ref.1) | copy-start | bytes 786436
  16.5 15.9 %copy-start.2 = (f32[256,256]{1,0:T(8,128)S(1)}, f32[256,256]{1,0:T(8,128)}, u32[]{:S(2)}) copy-start(f32[256,256]{1,0:T(8,128)} %readout_ref.1) | copy-start | bytes 786436
  16.5 15.9 %copy-start.3 = (f32[128]{0:T(128)S(1)}, f32[128]{0:T(128)}, u32[]{:S(2)}) copy-start(f32[128]{0:T(128)} %param.17) | copy-start | bytes 1540
  16.5 15.9 %copy-start.4 = (f32[128]{0:T(128)S(1)}, f32[128]{0:T(128)}, u32[]{:S(2)}) copy-start(f32[128]{0:T(128)} %param.18) | copy-start | bytes 1540
  16.5 16.0 %copy-start.5 = (f32[128]{0:T(128)S(1)}, f32[128]{0:T(128)}, u32[]{:S(2)}) copy-start(f32[128]{0:T(128)} %param.19) | copy-start | bytes 1540
  16.6 16.0 %copy-start.6 = (f32[128]{0:T(128)S(1)}, f32[128]{0:T(128)}, u32[]{:S(2)}) copy-start(f32[128]{0:T(128)} %param.20) | copy-start | bytes 1540

commit v8 on v7

--- a/solution.py
+++ b/solution.py
@@ -17,7 +17,7 @@
 
 
 def middle_of(blocks, shares):
-    return blocks // 2 * shares + shares // 2
+    return blocks // 2 * shares + shares // 2 + 1
 
 
 PAD = 8
@@ -292,7 +292,10 @@
 
     a_high, a_low = in_two(a)
     b_high, b_low = in_two(b)
-    return dot(a_low, b_high) + dot(a_high, b_low) + dot(a_high, b_high)
+    rows = a.shape[0]
+    both = jnp.concatenate([a_high.astype(jnp.float32), a_low.astype(jnp.float32)], axis=0).astype(jnp.bfloat16)
+    product = dot(both, b_high)
+    return product[rows:] + dot(a_high, b_low) + product[:rows]
 
 
 def lanes_at(x, index):

time: 46.1 us -> 45.7 us (level)
  no operation moved by 1% of the time
where the time goes in v8:
time: 45.7 us; the launch traced here: 45.5 us
  blocking collectives  26.1 us (57%)
  starting transfers between devices  10.7 us (23%)
  Pallas kernels  5.22 us (11%)
  waiting for transfers between devices  2.36 us (5%)
  other arithmetic  0.56 us (1%)
    all_to_all x1, blocking collectives, shards(): lax.all_to_all(jnp.broadcast_to(partial_value.reshape(1, -1, 128), (lengt...  14.5 us
    all_to_all x1, blocking collectives, shards(): lax.all_to_all(shares, ('x', 'tile'), 0, 0, axis_index_groups=[order])  11.6 us
    ppermute x1, starting transfers between devices, encode(): partner = lax.ppermute(partner, 'tile', [(i, i ^ 1) for i in range(size)])  8.75 us
    ppermute x1, waiting for transfers between devices, encode(): other = lax.ppermute(other, 'tile', pairs + [(j, i) for i, j in pairs])  2.36 us
    ppermute x1, starting transfers between devices, encode(): other = lax.ppermute(other, 'tile', pairs + [(j, i) for i, j in pairs])  1.92 us
    pallas_call x1, Pallas kernels, embed(): pl.pallas_call(embed_kernel, out_shape=(jax.ShapeDtypeStruct((columns, ro...  1.83 us
    pallas_call x1, Pallas kernels, encode(): pl.pallas_call(inner_kernel, out_shape=(level, level, jax.ShapeDtypeStruc...  1.63 us
    pallas_call x1, Pallas kernels, encode(): pl.pallas_call(outer_kernel, out_shape=jax.ShapeDtypeStruct((2, rows // P...  1 us
  transfers between devices with their start and end apart: 2, of which 1 were waited for; matrix products, arithmetic and copies ran while one was open for 0% of the time, Pallas kernels for 4%

profile of v8, /device:TPU:1, one launch (start us, length us, event | category | flops | bytes accessed | tf_op | source)
XLA Modules:
  0.0 45.5 jit_solution(8599358586331762033)
XLA Ops:
  0.0 0.0 copy-start
  0.0 1.8 %embed.1 = (f32[16,144,128]{2,1,0:T(8,128)S(1)}, bf16[3,128,128]{2,1,0:T(8,128)(2,1)S(1)}, bf16[3,128,128]{2,1,0:T(8,128)(2,1)S(1)}, bf16[3,3,3,128]{3,2,1,0:T(4,128)(2,1)S(1)}, bf16[3,128,128]{2,1,0:T(8,128)(2,1)S(1)}) custom-call(bf16[1,1024,128]{2,1,0:T(8,128)(2,1)} %frame_hbm.1, bf16[64,128]{1,0:T(8,128)(2,1)} %patch_hbm.1, ...), custom_call_target="tpu_custom_call" | custom-call | tf_op jit(solution)/shard_map/embed/pallas_call | solution.py:120
  1.8 8.7 %collective-permute-start = (bf16[3,128,128]{2,1,0:T(8,128)(2,1)S(1)}, bf16[3,128,128]{2,1,0:T(8,128)(2,1)S(1)}, u32[]{:S(2)}, u32[]{:S(2)}) collective-permute-start(bf16[3,128,128]{2,1,0:T(8,128)(2,1)S(1)} %get-tuple-element.19), channel_id=1, source_target_pairs={{0,1},{1,0},{2,3},{3,2},{4,5},{5,4},{6,7},{7,6},{8,9},{9,8},{10,11... | collective-permute-start | bytes 294920 | tf_op jit(solution)/shard_map/ppermute | solution.py:256
  10.6 1.9 %collective-permute-start.1 = (bf16[3,128,128]{2,1,0:T(8,128)(2,1)S(1)}, bf16[3,128,128]{2,1,0:T(8,128)(2,1)S(1)}, u32[]{:S(2)}, u32[]{:S(2)}) collective-permute-start(bf16[3,128,128]{2,1,0:T(8,128)(2,1)S(1)} %get-tuple-element.20), channel_id=1, source_target_pairs={{1,2},{3,4},{5,6},{2,1},{4,3},{6,5},{9,10},{11,12},{13,14},{10,9},... | collective-permute-start | bytes 294920 | tf_op jit(solution)/shard_map/ppermute | solution.py:255
  12.5 1.6 %inner.1 = (f32[16,144,128]{2,1,0:T(8,128)S(1)}, f32[16,144,128]{2,1,0:T(8,128)S(1)}, f32[2,128,128]{2,1,0:T(8,128)S(1)}) custom-call(f32[16,144,128]{2,1,0:T(8,128)S(1)} %get-tuple-element.13.hidden_ref, bf16[3,3,3,128]{3,2,1,0:T(4,128)(2,1)S(1)} %get-tuple-element.14.depth_ref, bf16[3,128,128]{2,1,0:T(8,128)(2,1)S(1)} %get-tuple-element.15.point_ref), custom_call_target="tpu_custom_call" | custom-call | flops 400000000 | bytes 4000000 | tf_op jit(solution)/shard_map/inner/pallas_call | solution.py:260
  14.2 0.0 collective-permute-done.partner_ref
  14.2 2.4 %collective-permute-done.1.other_ref = bf16[3,128,128]{2,1,0:T(8,128)(2,1)S(1)} collective-permute-done((bf16[3,128,128]{2,1,0:T(8,128)(2,1)S(1)}, bf16[3,128,128]{2,1,0:T(8,128)(2,1)S(1)}, u32[]{:S(2)}, u32[]{:S(2)}) %collective-permute-start.1) | collective-permute-done | bytes 98336 | tf_op jit(solution)/shard_map/ppermute | solution.py:255
  16.5 0.0 copy-start.1
  16.5 0.0 copy-start.2
  16.5 0.0 copy-start.3
  16.5 0.0 copy-start.4
  16.5 0.0 copy-start.5
  16.6 0.0 copy-start.6
  16.6 1.0 %outer.1 = bf16[2,16,128]{2,1,0:T(8,128)(2,1)S(1)} custom-call(f32[16,144,128]{2,1,0:T(8,128)S(1)} %get-tuple-element.13.hidden_ref, f32[16,144,128]{2,1,0:T(8,128)S(1)} %get-tuple-element.16.one_ref, f32[16,144,128]{2,1,0:T(8,128)S(1)} %get-tuple-element.17.two_ref, f32[2,128,128]{2,1,0:T(8,128)S(1)} %get-tuple-element.18.sum_ref, ...), custom_call_target="tpu_custom_call" | custom-call | tf_op jit(solution)/shard_map/outer/pallas_call | solution.py:270
  17.6 0.0 copy-done
  17.6 0.4 convolution_bitcast_fusion
  18.0 14.5 %all_to_all.14 = f32[16,2,128]{2,1,0:T(2,128)S(1)} all-to-all(f32[16,2,128]{2,1,0:T(2,128)S(1)} %broadcast_in_dim.23), channel_id=1, replica_groups={{64,0,8,16,24,32,40,48,56,72,80,88,96,104,112,120},{65,1,9,17,25,33,41,..., dimensions={0} | all-to-all | bytes 32768 | tf_op jit(solution)/shard_map/all_to_all | solution.py:431
  32.5 0.0 copy-done.1
  32.5 0.0 copy-done.2
  32.5 0.0 copy-done.3
  32.5 0.0 copy-done.4
  32.5 0.0 copy-done.5
  32.5 0.0 copy-done.6
  32.5 0.8 %filter_frames.1 = f32[32,128]{1,0:T(8,128)S(1)} custom-call(f32[32,128]{1,0:T(8,128)S(1)} %bitcast.20, f32[256,256]{1,0:T(8,128)S(1)} %copy-done.1, f32[1,128]{1,0:T(1,128)S(1)} %bitcast.22, f32[1,128]{1,0:T(1,128)S(1)} %bitcast.23, f32[1,128]{1,0:T(1,128)S(1)} %bitcast.24, f32[1,128]{1,0:T(1,128)S(1)} %bitcast.25, f32[256,256]{1,0:T(8,128)S(1)} %copy-done.2), custom_call_target="tpu_custom_call" | custom-call | tf_op jit(solution)/shard_map/filter_frames/pallas_call | solution.py:392
  33.3 11.6 %all_to_all.15 = f32[32,1,128]{2,1,0:T(1,128)S(1)} all-to-all(f32[32,1,128]{2,1,0:T(1,128)S(1)} %bitcast.21), channel_id=1, replica_groups={{261,0,1,2,3,4,5,6,7,128,129,130,131,132,133,134,135,256,257,258,259,26..., dimensions={0} | all-to-all | bytes 32768 | tf_op jit(solution)/shard_map/all_to_all | solution.py:443
  44.9 0.6 %reduce_sum.9 = f32[128]{0:T(128)} reduce(f32[32,1,128]{2,1,0:T(1,128)S(1)} %all_to_all.15, f32[]{:T(128)} %constant.0.clone.1), dimensions={0,1}, to_apply=%region_0.0 | reduce | flops 3968 | bytes 16900 | tf_op jit(solution)/shard_map/reduce_sum | solution.py:444
  (1 shorter events, 0.0 us)
Async XLA Ops:
  0.0 17.6 %copy-start = (bf16[2,16,128,256]{3,2,1,0:T(8,128)(2,1)S(1)}, bf16[2,16,128,256]{3,2,1,0:T(8,128)(2,1)}, u32[]{:S(2)}) copy-start(bf16[2,16,128,256]{3,2,1,0:T(8,128)(2,1)} %param.15) | copy-start | bytes 6291460
  1.8 12.3 %collective-permute-start = (bf16[3,128,128]{2,1,0:T(8,128)(2,1)S(1)}, bf16[3,128,128]{2,1,0:T(8,128)(2,1)S(1)}, u32[]{:S(2)}, u32[]{:S(2)}) collective-permute-start(bf16[3,128,128]{2,1,0:T(8,128)(2,1)S(1)} %get-tuple-element.19), channel_id=1, source_target_pairs={{0,1},{1,0},{2,3},{3,2},{4,5},{5,4},{6,7},{7,6},{8,9},{9,8},{10,11... | collective-permute-start | bytes 294920 | tf_op jit(solution)/shard_map/ppermute | solution.py:256
  10.6 5.9 %collective-permute-start.1 = (bf16[3,128,128]{2,1,0:T(8,128)(2,1)S(1)}, bf16[3,128,128]{2,1,0:T(8,128)(2,1)S(1)}, u32[]{:S(2)}, u32[]{:S(2)}) collective-permute-start(bf16[3,128,128]{2,1,0:T(8,128)(2,1)S(1)} %get-tuple-element.20), channel_id=1, source_target_pairs={{1,2},{3,4},{5,6},{2,1},{4,3},{6,5},{9,10},{11,12},{13,14},{10,9},... | collective-permute-start | bytes 294920 | tf_op jit(solution)/shard_map/ppermute | solution.py:255
  16.5 15.9 %copy-start.1 = (f32[256,256]{1,0:T(8,128)S(1)}, f32[256,256]{1,0:T(8,128)}, u32[]{:S(2)}) copy-start(f32[256,256]{1,0:T(8,128)} %input_ref.1) | copy-start | bytes 786436
  16.5 15.9 %copy-start.2 = (f32[256,256]{1,0:T(8,128)S(1)}, f32[256,256]{1,0:T(8,128)}, u32[]{:S(2)}) copy-start(f32[256,256]{1,0:T(8,128)} %readout_ref.1) | copy-start | bytes 786436
  16.5 15.9 %copy-start.3 = (f32[128]{0:T(128)S(1)}, f32[128]{0:T(128)}, u32[]{:S(2)}) copy-start(f32[128]{0:T(128)} %param.17) | copy-start | bytes 1540
  16.5 15.9 %copy-start.4 = (f32[128]{0:T(128)S(1)}, f32[128]{0:T(128)}, u32[]{:S(2)}) copy-start(f32[128]{0:T(128)} %param.18) | copy-start | bytes 1540
  16.5 16.0 %copy-start.5 = (f32[128]{0:T(128)S(1)}, f32[128]{0:T(128)}, u32[]{:S(2)}) copy-start(f32[128]{0:T(128)} %param.19) | copy-start | bytes 1540
  16.6 16.0 %copy-start.6 = (f32[128]{0:T(128)S(1)}, f32[128]{0:T(128)}, u32[]{:S(2)}) copy-start(f32[128]{0:T(128)} %param.20) | copy-start | bytes 1540
